TPU v7x, 32 devices: a whole 2x2x4 slice. The times are simulated.
32 devices in a mesh: groups: 2 (over x), win: 8 (over z, y), gx: 2 (over core).
Axes of the slice: x: 2, y: 2, z: 4, core: 2. Of those that a mesh axis runs over, the one named last changes fastest.
Arguments:
- prev_states: float32 [16, 1024, 128], P(('groups', 'win'), 'gx'), parts along dimension 0, may hold values from -6 to 6
- timesteps: int32 [16], P(('groups', 'win')), parts along dimension 0, may hold values from 0 to 999
- step_sizes: float32 [16], P(('groups', 'win')), parts along dimension 0, may hold values from 0.1 to 0.3
- slide: int32 [1], replicated, may hold values from 1 to 8
- w_time: bfloat16 [256, 768], replicated, may hold values from -0.375 to 0.375
- w_ada: bfloat16 [1, 768, 4608], replicated, may hold values from -0.21875 to 0.21875
- w_in: bfloat16 [128, 768], replicated, may hold values from -0.5 to 0.5
- w_qkv: bfloat16 [1, 768, 2304], replicated, may hold values from -2 to 2
- w_proj: bfloat16 [1, 768, 768], replicated, may hold values from -0.21875 to 0.21875
- w_up: bfloat16 [1, 768, 3072], replicated, may hold values from -0.21875 to 0.21875
- w_down: bfloat16 [1, 3072, 768], replicated, may hold values from -0.109375 to 0.109375
- w_out: bfloat16 [768, 128], replicated, may hold values from -0.21875 to 0.21875
Outputs:
- states_out: float32 [16, 1024, 128], P(('groups', 'win'), 'gx'), parts along dimension 0
There are 2 independent parts, one for each index of `groups`. A program takes and returns all parts, laid end to end along the dimension named above; an argument that names none is the same for every part. Nothing has to cross between parts.
All inputs are finite; a program needn't handle non-finite values.
Results may differ from a plain program's by a relative error of at most 0.0043.
Values may be sent and summed in bfloat16 or wider, within the bound.
No kernel may reach another device: no remote copies, remote signals or barrier semaphores. Data moves between devices by JAX's collectives and lax.ppermute only.
A program may use at most 128 MiB of HBM per device.

v0:
```python
import functools
import math

import jax
import jax.numpy as jnp
from jax import lax
from jax.experimental import pallas as pl
from jax.experimental.pallas import tpu as pltpu
from jax.sharding import PartitionSpec as P

HEADS = 12
SWEEPS = 2
GY = 8
GZ = 8
REACH = 3
EPSILON = 1e-06
FAR = -(2.0**100)
LANES = 128
VMEM_LIMIT = 28 << 20
EMBED_PART = 128
QKV_TILE = 768
LEAD = 1
ATT_UNROLL = 4
PROJ_PART = 512
UP_TILE = 1536
DOWN_PART = 512
EARLY = 2
F32 = jnp.float32
BF16 = jnp.bfloat16


def dot(a, b):
    return lax.dot_general(a, b, (((1,), (0,)), ((), ())), preferred_element_type=F32)


def dot_t(a, b):
    return lax.dot_general(a, b, (((1,), (1,)), ((), ())), preferred_element_type=F32)


def layer_norm(values):
    centred = values - jnp.mean(values, axis=-1, keepdims=True)
    spread = jnp.mean(centred * centred, axis=-1, keepdims=True)
    return centred * lax.rsqrt(spread + EPSILON)


def silu(x):
    return x / (1.0 + jnp.exp(-x))


def gelu_of_half(half):
    rate = math.sqrt(2.0 / math.pi)
    inner = half * (2.0 * rate + (8.0 * rate * 0.044715) * (half * half))
    return half + half * jnp.tanh(inner)


def modulation_kernel(emb_ref, w_time_hbm, w_ada_hbm, mods_ref, w_time, w_ada, sems):
    parts, _, wide = w_ada.shape
    first = pltpu.make_async_copy(w_time_hbm, w_time, sems.at[0])
    first.start()
    blocks = []
    for i in range(parts):
        block = w_ada_hbm.at[:, pl.ds(i * wide, wide)]
        blocks.append(pltpu.make_async_copy(block, w_ada.at[i], sems.at[1 + i]))
        blocks[-1].start()
    first.wait()
    condition = silu(dot(emb_ref[...], w_time[...]))
    active = silu(condition).astype(BF16)
    for i in range(parts):
        blocks[i].wait()
        mods_ref[i] = dot(active, w_ada[i])


def in_hbm(x):
    return pltpu.with_memory_space_constraint(x, pltpu.HBM)


def modulation(moment, w_time, w_ada):
    half = w_time.shape[0] // 2
    freqs = jnp.exp(-math.log(10000.0) * jnp.arange(half, dtype=F32) / half)
    angles = moment.astype(F32) * freqs
    embedded = jnp.concatenate([jnp.cos(angles), jnp.sin(angles)]).astype(BF16)
    embedded = jnp.broadcast_to(embedded[None], (8, embedded.shape[0]))
    parts = 6
    depth, wide = w_ada.shape
    vmem = pl.BlockSpec(memory_space=pltpu.VMEM)
    hbm = pl.BlockSpec(memory_space=pltpu.HBM)
    return pl.pallas_call(
        modulation_kernel,
        in_specs=[vmem, hbm, hbm],
        out_specs=vmem,
        out_shape=jax.ShapeDtypeStruct((parts, 8, wide // parts), F32),
        scratch_shapes=[
            pltpu.VMEM(w_time.shape, w_time.dtype),
            pltpu.VMEM((parts, depth, wide // parts), w_ada.dtype),
            pltpu.SemaphoreType.DMA((1 + parts,)),
        ],
        compiler_params=pltpu.CompilerParams(vmem_limit_bytes=16 << 20),
        cost_estimate=pl.CostEstimate(
            flops=16 * w_ada.size, bytes_accessed=2 * w_ada.size, transcendentals=0
        ),
        name="modulation",
    )(embedded, in_hbm(w_time), in_hbm(w_ada))


def first_sweep_kernel(halo_right, halo_left, *refs):
    fields, sources, incs, kept, rest = refs[:4], refs[4:10], refs[10:11], refs[11:17], refs[17:]
    scratch, sems = rest[:-1], rest[-1]
    copies = [
        pltpu.make_async_copy(source, target, sems.at[i])
        for i, (source, target) in enumerate(zip(sources, kept))
    ]
    for i in range(EARLY):
        copies[i].start()
    sweep_kernel(halo_right, halo_left, *fields, *kept, *incs, *scratch, arrived=copies)


def sweep_kernel(
    halo_right, halo_left,
    own_ref, halo_ref, mods_ref, step_ref,
    w_in, w_qkv, w_proj, w_up, w_down, w_out,
    inc_ref,
    h_scr, a_scr, b_scr, q_scr, k_scr, v_scr, o_scr, g_scr, qmask, kmask,
    arrived=None,
):
    def need(i):
        if arrived is not None:
            arrived[i].wait()
            if i == EARLY - 1:
                for copy in arrived[EARLY:]:
                    copy.start()

    rows, width = h_scr.shape
    rim = REACH * GY * GZ
    head = width // HEADS
    shift1, scale1 = mods_ref[0, 0:1, :], 1.0 + mods_ref[1, 0:1, :]
    shift2, scale2 = 0.5 * mods_ref[3, 0:1, :], 0.5 + 0.5 * mods_ref[4, 0:1, :]

    def place_of(shape):
        r = lax.broadcasted_iota(jnp.int32, shape, 0)
        f = lax.broadcasted_iota(jnp.int32, shape, 1)
        return f, r // (GY * GZ), (r // GZ) % GY, r % GZ

    f, plane, y, z = place_of(qmask.shape)
    hit = (f == y) | (f == GY + z) | (f == GY + GZ + plane)
    qmask[...] = jnp.where(hit, FAR, 0.0).astype(BF16)
    keys = kmask.shape[0]
    f, plane, y, z = place_of((GY * GZ, LANES))
    hit = (f == (y + GY // 2) % GY) | (f == GY + (z + GZ // 2) % GZ)
    near = jnp.where(hit, 1.0, 0.0).astype(BF16)
    end = jnp.where(f == GY + GZ, 1.0, 0.0).astype(BF16)
    start = jnp.where(f == GY + GZ + 1, 1.0, 0.0).astype(BF16)
    for p in range(2 * REACH + 2):
        more = {0: start, 2 * REACH + 1: end}.get(p)
        kmask[p * GY * GZ:(p + 1) * GY * GZ, :] = near if more is None else near + more

    need(0)

    def embed(x):
        h = dot(x, w_in[...])
        return h, (layer_norm(h) * scale1 + shift1).astype(BF16)

    a_scr[0:rim, :] = embed(halo_ref[halo_left:halo_left + rim, :])[1]
    a_scr[rim + rows:, :] = embed(halo_ref[halo_right:halo_right + rim, :])[1]
    for i in range(0, rows, EMBED_PART):
        h_scr[i:i + EMBED_PART, :], a_scr[rim + i:rim + i + EMBED_PART, :] = embed(
            own_ref[i:i + EMBED_PART, :]
        )

    need(1)
    unit = 1.0 / (math.sqrt(head) * math.log(2.0))

    @pl.loop(0, width // QKV_TILE)
    def _(j):
        at = pl.ds(pl.multiple_of(j * QKV_TILE, QKV_TILE), QKV_TILE)
        at_k = pl.ds(pl.multiple_of(width + j * QKV_TILE, QKV_TILE), QKV_TILE)
        at_v = pl.ds(pl.multiple_of(2 * width + j * QKV_TILE, QKV_TILE), QKV_TILE)
        q_scr[:, at] = (dot(a_scr[rim:rim + rows, :], w_qkv[:, at]) * unit).astype(BF16)
        k_scr[:, at] = dot(a_scr[...], w_qkv[:, at_k]).astype(BF16)
        v_scr[:, at] = dot(a_scr[...], w_qkv[:, at_v]).astype(BF16)

    lane = lax.broadcasted_iota(jnp.int32, (LANES, LANES), 1)
    first = lane < head

    @pl.loop(0, rows // LANES, unroll=ATT_UNROLL)
    def _(i):
        at = pl.ds(pl.multiple_of(i * LANES, LANES), LANES)
        window = pl.ds(pl.multiple_of(i * LANES, LANES), keys)
        qm = qmask[...]
        km = kmask[...]
        ones = jnp.ones((keys, LANES), BF16)
        zero = jnp.zeros((LANES, LANES), BF16)

        def scores(p):
            cols = slice(p * LANES, (p + 1) * LANES)
            q = q_scr[at, cols]
            qx = jnp.concatenate(
                [
                    jnp.concatenate([jnp.where(first, q, zero), qm], axis=1),
                    jnp.concatenate([jnp.where(first, zero, q), qm], axis=1),
                ],
                axis=0,
            )
            return dot_t(qx, jnp.concatenate([k_scr[window, cols], km], axis=1))

        def mix(p, s):
            cols = slice(p * LANES, (p + 1) * LANES)
            e = jnp.exp2(s - jnp.max(s, axis=-1, keepdims=True)).astype(BF16)
            o = dot(e, jnp.concatenate([v_scr[window, cols], ones], axis=1))
            num = jnp.where(first, o[:LANES, :LANES], o[LANES:, :LANES])
            den = jnp.where(first, o[:LANES, LANES:], o[LANES:, LANES:])
            o_scr[at, cols] = (num / den).astype(BF16)

        units = width // LANES
        waiting = [scores(p) for p in range(LEAD)]
        for p in range(units):
            if p + LEAD < units:
                waiting.append(scores(p + LEAD))
            mix(p, waiting.pop(0))

    need(2)
    for i in range(0, rows, PROJ_PART):
        at = slice(i, i + PROJ_PART)
        h = h_scr[at, :] + mods_ref[2, 0:1, :] * dot(o_scr[at, :], w_proj[...])
        h_scr[at, :] = h
        b_scr[at, :] = (layer_norm(h) * scale2 + shift2).astype(BF16)

    need(3)

    @pl.loop(0, w_up.shape[1] // UP_TILE)
    def _(j):
        at = pl.ds(pl.multiple_of(j * UP_TILE, UP_TILE), UP_TILE)
        g_scr[:, at] = gelu_of_half(dot(b_scr[...], w_up[:, at])).astype(BF16)

    need(4)
    need(5)
    step = step_ref[0]
    for i in range(0, rows, DOWN_PART):
        at = slice(i, i + DOWN_PART)
        h = h_scr[at, :] + mods_ref[5, 0:1, :] * dot(g_scr[at, :], w_down[...])
        out = step * dot(layer_norm(h).astype(BF16), w_out[...])
        inc_ref[at, :] = out


def sweep(own, halo, halo_right, halo_left, mods, step, weights, first):
    rows, channels = own.shape
    width, wide = weights[3].shape
    rim = REACH * GY * GZ
    full = rows + 2 * rim
    vmem = pl.BlockSpec(memory_space=pltpu.VMEM)
    hbm = pl.BlockSpec(memory_space=pltpu.HBM)
    scratch = [
        pltpu.VMEM((rows, width), F32),
        pltpu.VMEM((full, width), BF16),
        pltpu.VMEM((rows, width), BF16),
        pltpu.VMEM((rows, width), BF16),
        pltpu.VMEM((full, width), BF16),
        pltpu.VMEM((full, width), BF16),
        pltpu.VMEM((rows, width), BF16),
        pltpu.VMEM((rows, wide), BF16),
        pltpu.VMEM((LANES, LANES), BF16),
        pltpu.VMEM(((2 * REACH + 2) * GY * GZ, LANES), BF16),
    ]
    out_shape = [jax.ShapeDtypeStruct((rows, channels), F32)]
    kernel = sweep_kernel
    if first:
        kernel = first_sweep_kernel
        scratch.append(pltpu.SemaphoreType.DMA((len(weights),)))
        out_shape += [pltpu.VMEM(w.shape, w.dtype) for w in weights]
        weights = tuple(in_hbm(w) for w in weights)
    inc, *kept = pl.pallas_call(
        functools.partial(kernel, halo_right, halo_left),
        in_specs=[vmem, vmem, vmem, pl.BlockSpec(memory_space=pltpu.SMEM)]
        + [hbm if first else vmem] * len(weights),
        out_specs=[vmem] * len(out_shape),
        out_shape=out_shape,
        scratch_shapes=scratch,
        compiler_params=pltpu.CompilerParams(vmem_limit_bytes=VMEM_LIMIT),
        cost_estimate=pl.CostEstimate(
            flops=2 * rows * width * (4 * width + 2 * wide),
            bytes_accessed=sum(w.size * 2 for w in weights),
            transcendentals=0,
        ),
        name="first_sweep" if first else "sweep",
    )(own, halo, mods, step, *weights)
    return inc, tuple(kept) if first else weights


def rim_of_neighbours(field):
    count = lax.axis_size("gx")
    rows = field.shape[0]
    rim = REACH * GY * GZ
    if count == 2:
        other = lax.ppermute(field, "gx", [(0, 1), (1, 0)])
        return other, 0, rows - rim
    right = lax.ppermute(field[:rim], "gx", [((i + 1) % count, i) for i in range(count)])
    left = lax.ppermute(field[-rim:], "gx", [(i, (i + 1) % count) for i in range(count)])
    return jnp.concatenate([right, left]), 0, rim


def swap(x, distance):
    count = lax.axis_size("win")
    return lax.ppermute(x, "win", [(i, i ^ distance) for i in range(count)])


def together(*values):
    return lax.optimization_barrier(values)


def small_call(kernel, args, out_shape):
    vmem = pl.BlockSpec(memory_space=pltpu.VMEM)
    smem = pl.BlockSpec(memory_space=pltpu.SMEM)
    return pl.pallas_call(
        kernel,
        in_specs=[smem if x.dtype == jnp.int32 else vmem for x in args],
        out_specs=jax.tree.map(lambda _: vmem, out_shape),
        out_shape=out_shape,
        compiler_params=pltpu.CompilerParams(vmem_limit_bytes=4 << 20),
    )(*args)


def decisions(offset):
    count = lax.axis_size("win")
    place = lax.axis_index("win")
    bit = jnp.arange(count.bit_length() - 1, dtype=jnp.int32)
    distance = jnp.left_shift(1, bit)
    low = place & (distance - 1)
    mine = jnp.right_shift(place, bit) & 1
    lands = jnp.right_shift(mine * distance + low - offset, bit) & 1
    last = count // distance - 1 - jnp.right_shift(offset, bit)
    clamped = (low == distance - 1) & (jnp.right_shift(place, bit) >= last)
    keep = jnp.where(clamped, mine == 1, lands == mine)
    near = (jnp.right_shift(place ^ offset, bit) & 1) == 0
    return jnp.concatenate([keep, near, mine == 1]).astype(jnp.int32)


def pick(flags, flag, own, other):
    def kernel(flags_ref, own_ref, other_ref, out_ref):
        out_ref[...] = jnp.where(flags_ref[flag] != 0, own_ref[...], other_ref[...])

    return small_call(kernel, (flags, own, other), jax.ShapeDtypeStruct(own.shape, own.dtype))


def add_block(flags, flag, before, total, other):
    def kernel(flags_ref, *refs):
        *before_refs, total_ref, other_ref, before_out, total_out, sent_out = refs
        arrived = other_ref[...].astype(F32)
        mine = jnp.where(flags_ref[flag] != 0, arrived, 0.0)
        before_out[...] = before_refs[0][...] + mine if before_refs else mine
        sums = total_ref[...] + arrived
        total_out[...] = sums
        sent_out[...] = sums.astype(BF16)

    wide = jax.ShapeDtypeStruct(total.shape, F32)
    narrow = jax.ShapeDtypeStruct(total.shape, BF16)
    args = (flags,) + (() if before is None else (before,)) + (total, other)
    return small_call(kernel, args, (wide, wide, narrow))


def add_last(flags, flag, before, other, extra, kind):
    def kernel(flags_ref, before_ref, other_ref, *refs):
        mine = jnp.where(flags_ref[flag] != 0, other_ref[...].astype(F32), 0.0)
        total = before_ref[...] + mine
        for ref in refs[:-1]:
            total = total + ref[...]
        refs[-1][...] = total.astype(kind)

    return small_call(
        kernel, (flags, before, other) + extra,
        jax.ShapeDtypeStruct(before.shape, kind),
    )


def window_steps(
    prev_states, timesteps, step_sizes, slide,
    w_time, w_ada, w_in, w_qkv, w_proj, w_up, w_down, w_out,
):
    count = lax.axis_size("win")
    bits = count.bit_length() - 1
    assert count == 1 << bits and bits > 1, "window size"
    weights = (w_in, w_qkv[0], w_proj[0], w_up[0], w_down[0], w_out)
    flags = decisions(slide[0] - 1)
    mods = modulation(timesteps[0], w_time, w_ada[0])
    opening = prev_states[0]
    field = opening.astype(BF16)

    for bit in reversed(range(bits)):
        other = swap(field, 1 << bit)
        if bit == bits - 1:
            moved = swap(opening, 1)
            other, mods = together(other, mods)
        if bit == 0:
            field, opening, moved = together(field, opening, moved)
            opening = pick(flags, bits, opening, moved)
            moved = swap(opening, count // 2)
        field = pick(flags, bit, field, other)
    for sweep_index in range(SWEEPS):
        first = sweep_index == 0
        final = sweep_index == SWEEPS - 1
        halo, right, left = rim_of_neighbours(field)
        inc, weights = sweep(field, halo, right, left, mods, step_sizes, weights, first)
        if first:
            inc, opening, moved = together(inc, opening, moved)
            opening = pick(flags, 2 * bits - 1, opening, moved)
        before, total, sent = None, inc, inc.astype(BF16)
        for bit in range(bits - 1):
            other = swap(sent, 1 << bit)
            if first and bit + 1 < bits - 1:
                moved = swap(opening, 2 << bit)
                opening = pick(flags, bits + bit + 1, opening, moved)
            before, total, sent = add_block(flags, 2 * bits + bit, before, total, other)
        other = swap(sent, count // 2)
        field = add_last(
            flags, 3 * bits - 1, before, other, (opening, inc) if final else (opening,),
            F32 if final else BF16,
        )
    return field[None]


def solution(mesh):
    in_specs = (
        P(("groups", "win"), "gx", None), P(("groups", "win")), P(("groups", "win")),
        P(), P(), P(), P(), P(), P(), P(), P(), P(),
    )
    out_specs = P(("groups", "win"), "gx", None)
    return jax.shard_map(
        window_steps, mesh=mesh, in_specs=in_specs, out_specs=out_specs, check_vma=False
    )
```

profile of v0, /device:TPU:0, one launch (start us, length us, event | category | flops | bytes accessed | tf_op | source)
XLA Modules:
  0.0 105.7 jit_solution(5919486848737079400)
XLA Ops:
  0.0 1.0 bitcast_convert_fusion.own_ref
  1.0 4.1 %collective-permute-start = (bf16[512,128]{1,0:T(8,128)(2,1)S(1)}, bf16[512,128]{1,0:T(8,128)(2,1)S(1)}, u32[]{:S(2)}, u32[]{:S(2)}) collective-permute-start(bf16[512,128]{1,0:T(8,128)(2,1)S(1)} %bitcast_convert_fusion.own_ref), channel_id=1, source_target_pairs={{0,8},{2,10},{4,12},{6,14},{8,0},{10,2},{12,4},{14,6},{1,9},{3,11}... | collective-permute-start | bytes 393224 | tf_op jit(solution)/shard_map/ppermute | solution.py:302
  5.2 1.5 %collective-permute-start.2 = (f32[512,128]{1,0:T(8,128)}, f32[512,128]{1,0:T(8,128)S(1)}, u32[]{:S(2)}, u32[]{:S(2)}) collective-permute-start(f32[512,128]{1,0:T(8,128)} %bitcast.10), channel_id=1, source_target_pairs={{0,2},{2,0},{4,6},{6,4},{8,10},{10,8},{12,14},{14,12},{1,3},{3,1},... | collective-permute-start | bytes 786440 | tf_op jit(solution)/shard_map/ppermute | solution.py:302
  8.2 3.6 %modulation.1.refs_2_.mods_ref = f32[6,8,768]{2,1,0:T(8,128)S(1)} custom-call(bf16[8,256]{1,0:T(8,128)(2,1)S(1)} %broadcast_in_dim.4.emb_ref, bf16[256,768]{1,0:T(8,128)(2,1)} %w_time_hbm.1, bf16[768,4608]{1,0:T(8,128)(2,1)} %bitcast.12), custom_call_target="tpu_custom_call" | custom-call | flops 56623104 | bytes 7077888 | tf_op jit(solution)/shard_map/modulation/pallas_call | solution.py:87
  11.9 0.6 shard_map.118.own_ref
  12.5 1.6 %collective-permute-start.1 = (bf16[512,128]{1,0:T(8,128)(2,1)S(1)}, bf16[512,128]{1,0:T(8,128)(2,1)S(1)}, u32[]{:S(2)}, u32[]{:S(2)}) collective-permute-start(bf16[512,128]{1,0:T(8,128)(2,1)S(1)} %shard_map.118.own_ref), channel_id=1, source_target_pairs={{0,4},{2,6},{4,0},{6,2},{8,12},{10,14},{12,8},{14,10},{1,5},{3,7},... | collective-permute-start | bytes 393224 | tf_op jit(solution)/shard_map/ppermute | solution.py:302
  14.1 3.4 %collective-permute-done.1.other_ref = bf16[512,128]{1,0:T(8,128)(2,1)S(1)} collective-permute-done((bf16[512,128]{1,0:T(8,128)(2,1)S(1)}, bf16[512,128]{1,0:T(8,128)(2,1)S(1)}, u32[]{:S(2)}, u32[]{:S(2)}) %collective-permute-start.1) | collective-permute-done | bytes 131104 | tf_op jit(solution)/shard_map/ppermute | solution.py:302
  18.1 1.2 %collective-permute-start.3 = (bf16[512,128]{1,0:T(8,128)(2,1)S(1)}, bf16[512,128]{1,0:T(8,128)(2,1)S(1)}, u32[]{:S(2)}, u32[]{:S(2)}) collective-permute-start(bf16[512,128]{1,0:T(8,128)(2,1)S(1)} %shard_map.119.own_ref), channel_id=1, source_target_pairs={{0,2},{2,0},{4,6},{6,4},{8,10},{10,8},{12,14},{14,12},{1,3},{3,1},... | collective-permute-start | bytes 393224 | tf_op jit(solution)/shard_map/ppermute | solution.py:302
  19.3 3.8 %collective-permute-done.3.other_ref = bf16[512,128]{1,0:T(8,128)(2,1)S(1)} collective-permute-done((bf16[512,128]{1,0:T(8,128)(2,1)S(1)}, bf16[512,128]{1,0:T(8,128)(2,1)S(1)}, u32[]{:S(2)}, u32[]{:S(2)}) %collective-permute-start.3) | collective-permute-done | bytes 131104 | tf_op jit(solution)/shard_map/ppermute | solution.py:302
  25.0 2.5 %collective-permute-start.5 = (f32[512,128]{1,0:T(8,128)S(1)}, f32[512,128]{1,0:T(8,128)S(1)}, u32[]{:S(2)}, u32[]{:S(2)}) collective-permute-start(f32[512,128]{1,0:T(8,128)S(1)} %shard_map.121.own_ref), channel_id=1, source_target_pairs={{0,8},{2,10},{4,12},{6,14},{8,0},{10,2},{12,4},{14,6},{1,9},{3,11}... | collective-permute-start | bytes 786440 | tf_op jit(solution)/shard_map/ppermute | solution.py:302
  27.5 18.0 %first_sweep.1 = (f32[512,128]{1,0:T(8,128)S(1)}, bf16[128,768]{1,0:T(8,128)(2,1)S(1)}, bf16[768,2304]{1,0:T(8,128)(2,1)S(1)}, bf16[768,768]{1,0:T(8,128)(2,1)S(...) custom-call(bf16[512,128]{1,0:T(8,128)(2,1)S(1)} %shard_map.120.refs_0_, ...), custom_call_target="tpu_custom_call" | custom-call | flops 7247757312 | bytes 14548992 | tf_op jit(solution)/shard_map/first_sweep/pallas_call | solution.py:270
  45.6 1.6 %collective-permute-start.6 = (bf16[512,128]{1,0:T(8,128)(2,1)S(1)}, bf16[512,128]{1,0:T(8,128)(2,1)S(1)}, u32[]{:S(2)}, u32[]{:S(2)}) collective-permute-start(bf16[512,128]{1,0:T(8,128)(2,1)S(1)} %convert_element_type.27), channel_id=1, source_target_pairs={{0,2},{2,0},{4,6},{6,4},{8,10},{10,8},{12,14},{14,12},{1,3},{3,1},... | collective-permute-start | bytes 393224 | tf_op jit(solution)/shard_map/ppermute | solution.py:302
  47.1 4.1 %collective-permute-done.6.refs_1_ = bf16[512,128]{1,0:T(8,128)(2,1)S(1)} collective-permute-done((bf16[512,128]{1,0:T(8,128)(2,1)S(1)}, bf16[512,128]{1,0:T(8,128)(2,1)S(1)}, u32[]{:S(2)}, u32[]{:S(2)}) %collective-permute-start.6) | collective-permute-done | bytes 131104 | tf_op jit(solution)/shard_map/ppermute | solution.py:302
  51.2 0.6 shard_map.122
  51.8 1.8 %collective-permute-start.7 = (bf16[512,128]{1,0:T(8,128)(2,1)S(1)}, bf16[512,128]{1,0:T(8,128)(2,1)S(1)}, u32[]{:S(2)}, u32[]{:S(2)}) collective-permute-start(bf16[512,128]{1,0:T(8,128)(2,1)S(1)} %get-tuple-element.39), channel_id=1, source_target_pairs={{0,4},{2,6},{4,0},{6,2},{8,12},{10,14},{12,8},{14,10},{1,5},{3,7},... | collective-permute-start | bytes 393224 | tf_op jit(solution)/shard_map/ppermute | solution.py:302
  54.6 3.2 %collective-permute-done.7.refs_2_ = bf16[512,128]{1,0:T(8,128)(2,1)S(1)} collective-permute-done((bf16[512,128]{1,0:T(8,128)(2,1)S(1)}, bf16[512,128]{1,0:T(8,128)(2,1)S(1)}, u32[]{:S(2)}, u32[]{:S(2)}) %collective-permute-start.7) | collective-permute-done | bytes 131104 | tf_op jit(solution)/shard_map/ppermute | solution.py:302
  57.8 1.3 %shard_map.123 = (f32[512,128]{1,0:T(8,128)S(1)}, f32[512,128]{1,0:T(8,128)}, bf16[512,128]{1,0:T(8,128)(2,1)S(1)}) custom-call(s32[9]{0:T(128)S(1)} %add_convert_fusion.flags_ref, f32[512,128]{1,0:T(8,128)S(1)} %get-tuple-element.37.refs_0_, f32[512,128]{1,0:T(8,128)S(1)} %get-tuple-element.38.refs_1_, bf16[512,128]{1,0:T(8,128)(2,1)S(1)} %collective-permute-done.7.refs_2_), custom_call_target="tpu_custom_call" | custom-call | tf_op jit(solution)/shard_map/pallas_call | solution.py:312
  59.1 0.7 collective-permute-start.8
  59.8 4.2 %collective-permute-done.9.other_ref = f32[512,128]{1,0:T(8,128)S(1)} collective-permute-done((f32[512,128]{1,0:T(8,128)S(1)}, f32[512,128]{1,0:T(8,128)S(1)}, u32[]{:S(2)}, u32[]{:S(2)}) %collective-permute-start.9) | collective-permute-done | bytes 262176 | tf_op jit(solution)/shard_map/ppermute | solution.py:302
  64.5 0.8 collective-permute-done.8.other_ref
  65.3 0.6 shard_map.126.own_ref
  66.0 1.3 %collective-permute-done.10.halo_ref = bf16[512,128]{1,0:T(8,128)(2,1)S(1)} collective-permute-done((bf16[512,128]{1,0:T(8,128)(2,1)S(1)}, bf16[512,128]{1,0:T(8,128)(2,1)S(1)}, u32[]{:S(2)}, u32[]{:S(2)}) %collective-permute-start.10) | collective-permute-done | bytes 131104 | tf_op jit(solution)/shard_map/ppermute | solution.py:293
  67.3 16.3 %sweep.1.refs_0_.refs_1_ = f32[512,128]{1,0:T(8,128)S(1)} custom-call(bf16[512,128]{1,0:T(8,128)(2,1)S(1)} %shard_map.126.own_ref, bf16[512,128]{1,0:T(8,128)(2,1)S(1)} %collective-permute-done.10.halo_ref, f32[6,8,768]{2,1,0:T(8,128)S(1)} %modulation.1.refs_2_.mods_ref, f32[1]{0:T(128)S(6)} %copy.14.refs_3_.step_ref, ...), custom_call_target="tpu_custom_call" | custom-call | flops 7247757312 | bytes 14548992 | tf_op jit(solution)/shard_map/sweep/pallas_call | solution.py:270
  83.6 2.2 %collective-permute-start.11 = (bf16[512,128]{1,0:T(8,128)(2,1)S(1)}, bf16[512,128]{1,0:T(8,128)(2,1)S(1)}, u32[]{:S(2)}, u32[]{:S(2)}) collective-permute-start(bf16[512,128]{1,0:T(8,128)(2,1)S(1)} %convert_element_type.28), channel_id=1, source_target_pairs={{0,2},{2,0},{4,6},{6,4},{8,10},{10,8},{12,14},{14,12},{1,3},{3,1},... | collective-permute-start | bytes 393224 | tf_op jit(solution)/shard_map/ppermute | solution.py:302
  85.8 3.8 %collective-permute-done.11.refs_1_ = bf16[512,128]{1,0:T(8,128)(2,1)S(1)} collective-permute-done((bf16[512,128]{1,0:T(8,128)(2,1)S(1)}, bf16[512,128]{1,0:T(8,128)(2,1)S(1)}, u32[]{:S(2)}, u32[]{:S(2)}) %collective-permute-start.11) | collective-permute-done | bytes 131104 | tf_op jit(solution)/shard_map/ppermute | solution.py:302
  89.6 0.6 shard_map.127
  90.2 1.6 %collective-permute-start.12 = (bf16[512,128]{1,0:T(8,128)(2,1)S(1)}, bf16[512,128]{1,0:T(8,128)(2,1)S(1)}, u32[]{:S(2)}, u32[]{:S(2)}) collective-permute-start(bf16[512,128]{1,0:T(8,128)(2,1)S(1)} %get-tuple-element.52), channel_id=1, source_target_pairs={{0,4},{2,6},{4,0},{6,2},{8,12},{10,14},{12,8},{14,10},{1,5},{3,7},... | collective-permute-start | bytes 393224 | tf_op jit(solution)/shard_map/ppermute | solution.py:302
  91.8 3.4 %collective-permute-done.12.refs_2_ = bf16[512,128]{1,0:T(8,128)(2,1)S(1)} collective-permute-done((bf16[512,128]{1,0:T(8,128)(2,1)S(1)}, bf16[512,128]{1,0:T(8,128)(2,1)S(1)}, u32[]{:S(2)}, u32[]{:S(2)}) %collective-permute-start.12) | collective-permute-done | bytes 131104 | tf_op jit(solution)/shard_map/ppermute | solution.py:302
  95.2 1.3 %shard_map.128 = (f32[512,128]{1,0:T(8,128)S(1)}, f32[512,128]{1,0:T(8,128)}, bf16[512,128]{1,0:T(8,128)(2,1)S(1)}) custom-call(s32[9]{0:T(128)S(1)} %add_convert_fusion.flags_ref, f32[512,128]{1,0:T(8,128)S(1)} %get-tuple-element.50.refs_0_, f32[512,128]{1,0:T(8,128)S(1)} %get-tuple-element.51.refs_1_, bf16[512,128]{1,0:T(8,128)(2,1)S(1)} %collective-permute-done.12.refs_2_), custom_call_target="tpu_custom_call" | custom-call | tf_op jit(solution)/shard_map/pallas_call | solution.py:312
  96.5 2.2 %collective-permute-start.13 = (bf16[512,128]{1,0:T(8,128)(2,1)S(1)}, bf16[512,128]{1,0:T(8,128)(2,1)S(1)}, u32[]{:S(2)}, u32[]{:S(2)}) collective-permute-start(bf16[512,128]{1,0:T(8,128)(2,1)S(1)} %get-tuple-element.54), channel_id=1, source_target_pairs={{0,8},{2,10},{4,12},{6,14},{8,0},{10,2},{12,4},{14,6},{1,9},{3,11}... | collective-permute-start | bytes 393224 | tf_op jit(solution)/shard_map/ppermute | solution.py:302
  98.7 5.6 %collective-permute-done.13.other_ref = bf16[512,128]{1,0:T(8,128)(2,1)S(1)} collective-permute-done((bf16[512,128]{1,0:T(8,128)(2,1)S(1)}, bf16[512,128]{1,0:T(8,128)(2,1)S(1)}, u32[]{:S(2)}, u32[]{:S(2)}) %collective-permute-start.13) | collective-permute-done | bytes 131104 | tf_op jit(solution)/shard_map/ppermute | solution.py:302
  104.4 1.3 %shard_map.129 = f32[512,128]{1,0:T(8,128)} custom-call(s32[9]{0:T(128)S(1)} %add_convert_fusion.flags_ref, f32[512,128]{1,0:T(8,128)S(1)} %get-tuple-element.53.before_ref, bf16[512,128]{1,0:T(8,128)(2,1)S(1)} %collective-permute-done.13.other_ref, f32[512,128]{1,0:T(8,128)S(1)} %shard_map.125.refs_0_, f32[512,128]{1,0:T(8,128)S(1)} %sweep.1.refs_0_.refs_1_), custom_call_target="tpu_custom_call" | custom-call | tf_op jit(solution)/shard_map/pallas_call | solution.py:312
  (22 shorter events, 3.7 us)
Async XLA Ops:
  0.0 24.4 %copy-start = (f32[1,512,128]{2,1,0:T(8,128)S(1)}, f32[1,512,128]{2,1,0:T(8,128)}, u32[]{:S(2)}) copy-start(f32[1,512,128]{2,1,0:T(8,128)} %param.12) | copy-start | bytes 786436
  1.0 10.8 %collective-permute-start = (bf16[512,128]{1,0:T(8,128)(2,1)S(1)}, bf16[512,128]{1,0:T(8,128)(2,1)S(1)}, u32[]{:S(2)}, u32[]{:S(2)}) collective-permute-start(bf16[512,128]{1,0:T(8,128)(2,1)S(1)} %bitcast_convert_fusion.own_ref), channel_id=1, source_target_pairs={{0,8},{2,10},{4,12},{6,14},{8,0},{10,2},{12,4},{14,6},{1,9},{3,11}... | collective-permute-start | bytes 393224 | tf_op jit(solution)/shard_map/ppermute | solution.py:302
  5.2 14.1 %collective-permute-start.2 = (f32[512,128]{1,0:T(8,128)}, f32[512,128]{1,0:T(8,128)S(1)}, u32[]{:S(2)}, u32[]{:S(2)}) collective-permute-start(f32[512,128]{1,0:T(8,128)} %bitcast.10), channel_id=1, source_target_pairs={{0,2},{2,0},{4,6},{6,4},{8,10},{10,8},{12,14},{14,12},{1,3},{3,1},... | collective-permute-start | bytes 786440 | tf_op jit(solution)/shard_map/ppermute | solution.py:302
  12.5 5.0 %collective-permute-start.1 = (bf16[512,128]{1,0:T(8,128)(2,1)S(1)}, bf16[512,128]{1,0:T(8,128)(2,1)S(1)}, u32[]{:S(2)}, u32[]{:S(2)}) collective-permute-start(bf16[512,128]{1,0:T(8,128)(2,1)S(1)} %shard_map.118.own_ref), channel_id=1, source_target_pairs={{0,4},{2,6},{4,0},{6,2},{8,12},{10,14},{12,8},{14,10},{1,5},{3,7},... | collective-permute-start | bytes 393224 | tf_op jit(solution)/shard_map/ppermute | solution.py:302
  18.1 5.0 %collective-permute-start.3 = (bf16[512,128]{1,0:T(8,128)(2,1)S(1)}, bf16[512,128]{1,0:T(8,128)(2,1)S(1)}, u32[]{:S(2)}, u32[]{:S(2)}) collective-permute-start(bf16[512,128]{1,0:T(8,128)(2,1)S(1)} %shard_map.119.own_ref), channel_id=1, source_target_pairs={{0,2},{2,0},{4,6},{6,4},{8,10},{10,8},{12,14},{14,12},{1,3},{3,1},... | collective-permute-start | bytes 393224 | tf_op jit(solution)/shard_map/ppermute | solution.py:302
  23.7 3.8 %collective-permute-start.4 = (bf16[512,128]{1,0:T(8,128)(2,1)S(1)}, bf16[512,128]{1,0:T(8,128)(2,1)S(1)}, u32[]{:S(2)}, u32[]{:S(2)}) collective-permute-start(bf16[512,128]{1,0:T(8,128)(2,1)S(1)} %shard_map.120.refs_0_), channel_id=1, source_target_pairs={{0,1},{1,0},{2,3},{3,2},{4,5},{5,4},{6,7},{7,6},{8,9},{9,8},{10,11... | collective-permute-start | bytes 393224 | tf_op jit(solution)/shard_map/ppermute | solution.py:293
  25.0 20.5 %collective-permute-start.5 = (f32[512,128]{1,0:T(8,128)S(1)}, f32[512,128]{1,0:T(8,128)S(1)}, u32[]{:S(2)}, u32[]{:S(2)}) collective-permute-start(f32[512,128]{1,0:T(8,128)S(1)} %shard_map.121.own_ref), channel_id=1, source_target_pairs={{0,8},{2,10},{4,12},{6,14},{8,0},{10,2},{12,4},{14,6},{1,9},{3,11}... | collective-permute-start | bytes 786440 | tf_op jit(solution)/shard_map/ppermute | solution.py:302
  45.6 5.7 %collective-permute-start.6 = (bf16[512,128]{1,0:T(8,128)(2,1)S(1)}, bf16[512,128]{1,0:T(8,128)(2,1)S(1)}, u32[]{:S(2)}, u32[]{:S(2)}) collective-permute-start(bf16[512,128]{1,0:T(8,128)(2,1)S(1)} %convert_element_type.27), channel_id=1, source_target_pairs={{0,2},{2,0},{4,6},{6,4},{8,10},{10,8},{12,14},{14,12},{1,3},{3,1},... | collective-permute-start | bytes 393224 | tf_op jit(solution)/shard_map/ppermute | solution.py:302
  51.8 5.9 %collective-permute-start.7 = (bf16[512,128]{1,0:T(8,128)(2,1)S(1)}, bf16[512,128]{1,0:T(8,128)(2,1)S(1)}, u32[]{:S(2)}, u32[]{:S(2)}) collective-permute-start(bf16[512,128]{1,0:T(8,128)(2,1)S(1)} %get-tuple-element.39), channel_id=1, source_target_pairs={{0,4},{2,6},{4,0},{6,2},{8,12},{10,14},{12,8},{14,10},{1,5},{3,7},... | collective-permute-start | bytes 393224 | tf_op jit(solution)/shard_map/ppermute | solution.py:302
  54.2 9.7 %collective-permute-start.9 = (f32[512,128]{1,0:T(8,128)S(1)}, f32[512,128]{1,0:T(8,128)S(1)}, u32[]{:S(2)}, u32[]{:S(2)}) collective-permute-start(f32[512,128]{1,0:T(8,128)S(1)} %shard_map.124.own_ref), channel_id=1, source_target_pairs={{0,4},{2,6},{4,0},{6,2},{8,12},{10,14},{12,8},{14,10},{1,5},{3,7},... | collective-permute-start | bytes 786440 | tf_op jit(solution)/shard_map/ppermute | solution.py:302
  59.1 6.2 %collective-permute-start.8 = (bf16[512,128]{1,0:T(8,128)(2,1)S(1)}, bf16[512,128]{1,0:T(8,128)(2,1)S(1)}, u32[]{:S(2)}, u32[]{:S(2)}) collective-permute-start(bf16[512,128]{1,0:T(8,128)(2,1)S(1)} %get-tuple-element.41), channel_id=1, source_target_pairs={{0,8},{2,10},{4,12},{6,14},{8,0},{10,2},{12,4},{14,6},{1,9},{3,11}... | collective-permute-start | bytes 393224 | tf_op jit(solution)/shard_map/ppermute | solution.py:302
  65.9 1.4 %collective-permute-start.10 = (bf16[512,128]{1,0:T(8,128)(2,1)S(1)}, bf16[512,128]{1,0:T(8,128)(2,1)S(1)}, u32[]{:S(2)}, u32[]{:S(2)}) collective-permute-start(bf16[512,128]{1,0:T(8,128)(2,1)S(1)} %shard_map.126.own_ref), channel_id=1, source_target_pairs={{0,1},{1,0},{2,3},{3,2},{4,5},{5,4},{6,7},{7,6},{8,9},{9,8},{10,11... | collective-permute-start | bytes 393224 | tf_op jit(solution)/shard_map/ppermute | solution.py:293
  83.6 6.0 %collective-permute-start.11 = (bf16[512,128]{1,0:T(8,128)(2,1)S(1)}, bf16[512,128]{1,0:T(8,128)(2,1)S(1)}, u32[]{:S(2)}, u32[]{:S(2)}) collective-permute-start(bf16[512,128]{1,0:T(8,128)(2,1)S(1)} %convert_element_type.28), channel_id=1, source_target_pairs={{0,2},{2,0},{4,6},{6,4},{8,10},{10,8},{12,14},{14,12},{1,3},{3,1},... | collective-permute-start | bytes 393224 | tf_op jit(solution)/shard_map/ppermute | solution.py:302
  90.2 5.0 %collective-permute-start.12 = (bf16[512,128]{1,0:T(8,128)(2,1)S(1)}, bf16[512,128]{1,0:T(8,128)(2,1)S(1)}, u32[]{:S(2)}, u32[]{:S(2)}) collective-permute-start(bf16[512,128]{1,0:T(8,128)(2,1)S(1)} %get-tuple-element.52), channel_id=1, source_target_pairs={{0,4},{2,6},{4,0},{6,2},{8,12},{10,14},{12,8},{14,10},{1,5},{3,7},... | collective-permute-start | bytes 393224 | tf_op jit(solution)/shard_map/ppermute | solution.py:302
  96.5 7.8 %collective-permute-start.13 = (bf16[512,128]{1,0:T(8,128)(2,1)S(1)}, bf16[512,128]{1,0:T(8,128)(2,1)S(1)}, u32[]{:S(2)}, u32[]{:S(2)}) collective-permute-start(bf16[512,128]{1,0:T(8,128)(2,1)S(1)} %get-tuple-element.54), channel_id=1, source_target_pairs={{0,8},{2,10},{4,12},{6,14},{8,0},{10,2},{12,4},{14,6},{1,9},{3,11}... | collective-permute-start | bytes 393224 | tf_op jit(solution)/shard_map/ppermute | solution.py:302
where the time goes:
time: 106 us
  Pallas kernels  47 us (44%)
  waiting for transfers between devices  33.7 us (32%)
  starting transfers between devices  21.5 us (20%)
  between operations  2.13 us (2%)
  other arithmetic  1.35 us (1%)
    pallas_call x2, Pallas kernels, sweep(): pl.pallas_call(functools.partial(kernel, halo_right, halo_left), in_specs...  34.3 us
    ppermute x12, waiting for transfers between devices, swap(): return lax.ppermute(x, 'win', [(i, i ^ distance) for i in range(count)])  32.4 us
    ppermute x12, starting transfers between devices, swap(): return lax.ppermute(x, 'win', [(i, i ^ distance) for i in range(count)])  21.4 us
    pallas_call x12, Pallas kernels, small_call(): pl.pallas_call(kernel, in_specs=[smem if x.dtype == jnp.int32 else vmem f...  9.11 us
    pallas_call x1, Pallas kernels, modulation(): pl.pallas_call(modulation_kernel, in_specs=[vmem, hbm, hbm], out_specs=vm...  3.57 us
  transfers between devices with their start and end apart: 14, of which 10 were waited for; matrix products, arithmetic and copies ran while one was open for 0% of the time, Pallas kernels for 24%

commit v1 on v0

--- a/solution.py
+++ b/solution.py
@@ -24,7 +24,6 @@
 PROJ_PART = 512
 UP_TILE = 1536
 DOWN_PART = 512
-EARLY = 2
 F32 = jnp.float32
 BF16 = jnp.bfloat16
 
@@ -72,6 +71,35 @@
 
 def in_hbm(x):
     return pltpu.with_memory_space_constraint(x, pltpu.HBM)
+
+
+def load_kernel(*refs):
+    count = len(refs) // 2
+    sems = refs[-1]
+    copies = [
+        pltpu.make_async_copy(refs[i], refs[count + i], sems.at[i]) for i in range(count)
+    ]
+    for copy in copies:
+        copy.start()
+    for copy in copies:
+        copy.wait()
+
+
+def load(arrays):
+    return tuple(
+        pl.pallas_call(
+            load_kernel,
+            in_specs=[pl.BlockSpec(memory_space=pltpu.HBM)] * len(arrays),
+            out_specs=[pl.BlockSpec(memory_space=pltpu.VMEM)] * len(arrays),
+            out_shape=[pltpu.VMEM(x.shape, x.dtype) for x in arrays],
+            scratch_shapes=[pltpu.SemaphoreType.DMA((len(arrays),))],
+            compiler_params=pltpu.CompilerParams(vmem_limit_bytes=4 << 20),
+            cost_estimate=pl.CostEstimate(
+                flops=0, bytes_accessed=sum(2 * x.size for x in arrays), transcendentals=0
+            ),
+            name="load",
+        )(*[in_hbm(x) for x in arrays])
+    )
 
 
 def modulation(moment, w_time, w_ada):
@@ -103,15 +131,13 @@
 
 
 def first_sweep_kernel(halo_right, halo_left, *refs):
-    fields, sources, incs, kept, rest = refs[:4], refs[4:10], refs[10:11], refs[11:17], refs[17:]
-    scratch, sems = rest[:-1], rest[-1]
-    copies = [
-        pltpu.make_async_copy(source, target, sems.at[i])
-        for i, (source, target) in enumerate(zip(sources, kept))
-    ]
-    for i in range(EARLY):
-        copies[i].start()
-    sweep_kernel(halo_right, halo_left, *fields, *kept, *incs, *scratch, arrived=copies)
+    fields, ready, sources, (inc,), kept = refs[:4], refs[4:6], refs[6:10], refs[10:11], refs[11:15]
+    scratch, sems = refs[15:-1], refs[-1]
+    copies = [None] * len(ready)
+    for i, (source, target) in enumerate(zip(sources, kept)):
+        copies.append(pltpu.make_async_copy(source, target, sems.at[i]))
+        copies[-1].start()
+    sweep_kernel(halo_right, halo_left, *fields, *ready, *kept, inc, *scratch, arrived=copies)
 
 
 def sweep_kernel(
@@ -123,11 +149,8 @@
     arrived=None,
 ):
     def need(i):
-        if arrived is not None:
+        if arrived is not None and arrived[i] is not None:
             arrived[i].wait()
-            if i == EARLY - 1:
-                for copy in arrived[EARLY:]:
-                    copy.start()
 
     rows, width = h_scr.shape
     rim = REACH * GY * GZ
@@ -264,13 +287,15 @@
     kernel = sweep_kernel
     if first:
         kernel = first_sweep_kernel
-        scratch.append(pltpu.SemaphoreType.DMA((len(weights),)))
-        out_shape += [pltpu.VMEM(w.shape, w.dtype) for w in weights]
-        weights = tuple(in_hbm(w) for w in weights)
+        late = weights[2:]
+        scratch.append(pltpu.SemaphoreType.DMA((len(late),)))
+        out_shape += [pltpu.VMEM(w.shape, w.dtype) for w in late]
+        weights = weights[:2] + tuple(in_hbm(w) for w in late)
     inc, *kept = pl.pallas_call(
         functools.partial(kernel, halo_right, halo_left),
         in_specs=[vmem, vmem, vmem, pl.BlockSpec(memory_space=pltpu.SMEM)]
-        + [hbm if first else vmem] * len(weights),
+        + [vmem] * 2
+        + [hbm if first else vmem] * (len(weights) - 2),
         out_specs=[vmem] * len(out_shape),
         out_shape=out_shape,
         scratch_shapes=scratch,
@@ -282,7 +307,7 @@
         ),
         name="first_sweep" if first else "sweep",
     )(own, halo, mods, step, *weights)
-    return inc, tuple(kept) if first else weights
+    return inc, weights[:2] + tuple(kept) if first else weights
 
 
 def rim_of_neighbours(field):
@@ -308,17 +333,16 @@
 
 def small_call(kernel, args, out_shape):
     vmem = pl.BlockSpec(memory_space=pltpu.VMEM)
-    smem = pl.BlockSpec(memory_space=pltpu.SMEM)
     return pl.pallas_call(
         kernel,
-        in_specs=[smem if x.dtype == jnp.int32 else vmem for x in args],
+        in_specs=[vmem] * len(args),
         out_specs=jax.tree.map(lambda _: vmem, out_shape),
         out_shape=out_shape,
         compiler_params=pltpu.CompilerParams(vmem_limit_bytes=4 << 20),
     )(*args)
 
 
-def decisions(offset):
+def decisions(offset, lanes):
     count = lax.axis_size("win")
     place = lax.axis_index("win")
     bit = jnp.arange(count.bit_length() - 1, dtype=jnp.int32)
@@ -330,35 +354,42 @@
     clamped = (low == distance - 1) & (jnp.right_shift(place, bit) >= last)
     keep = jnp.where(clamped, mine == 1, lands == mine)
     near = (jnp.right_shift(place ^ offset, bit) & 1) == 0
-    return jnp.concatenate([keep, near, mine == 1]).astype(jnp.int32)
+    flags = jnp.concatenate([keep, near, mine == 1]).astype(jnp.int32)
+    return jnp.broadcast_to(flags[:, None], (flags.shape[0], lanes))
 
 
 def pick(flags, flag, own, other):
     def kernel(flags_ref, own_ref, other_ref, out_ref):
-        out_ref[...] = jnp.where(flags_ref[flag] != 0, own_ref[...], other_ref[...])
+        own = flags_ref[flag:flag + 1, :] != 0
+        out_ref[...] = jnp.where(own, own_ref[...], other_ref[...])
 
     return small_call(kernel, (flags, own, other), jax.ShapeDtypeStruct(own.shape, own.dtype))
 
 
-def add_block(flags, flag, before, total, other):
+def add_block(flags, flag, before, total, other, more):
     def kernel(flags_ref, *refs):
-        *before_refs, total_ref, other_ref, before_out, total_out, sent_out = refs
-        arrived = other_ref[...].astype(F32)
-        mine = jnp.where(flags_ref[flag] != 0, arrived, 0.0)
-        before_out[...] = before_refs[0][...] + mine if before_refs else mine
-        sums = total_ref[...] + arrived
-        total_out[...] = sums
-        sent_out[...] = sums.astype(BF16)
+        refs = list(refs)
+        start = refs.pop(0)[...] if before is not None else 0.0
+        sums = refs[0][...]
+        arrived = refs[1][...].astype(F32)
+        above = flags_ref[flag:flag + 1, :] != 0
+        refs[2][...] = start + jnp.where(above, arrived, 0.0)
+        sums = sums + arrived
+        refs[3][...] = sums.astype(BF16)
+        if more:
+            refs[4][...] = sums
 
     wide = jax.ShapeDtypeStruct(total.shape, F32)
     narrow = jax.ShapeDtypeStruct(total.shape, BF16)
     args = (flags,) + (() if before is None else (before,)) + (total, other)
-    return small_call(kernel, args, (wide, wide, narrow))
+    out = small_call(kernel, args, (wide, narrow) + ((wide,) if more else ()))
+    return out if more else (*out, None)
 
 
 def add_last(flags, flag, before, other, extra, kind):
     def kernel(flags_ref, before_ref, other_ref, *refs):
-        mine = jnp.where(flags_ref[flag] != 0, other_ref[...].astype(F32), 0.0)
+        above = flags_ref[flag:flag + 1, :] != 0
+        mine = jnp.where(above, other_ref[...].astype(F32), 0.0)
         total = before_ref[...] + mine
         for ref in refs[:-1]:
             total = total + ref[...]
@@ -378,13 +409,15 @@
     bits = count.bit_length() - 1
     assert count == 1 << bits and bits > 1, "window size"
     weights = (w_in, w_qkv[0], w_proj[0], w_up[0], w_down[0], w_out)
-    flags = decisions(slide[0] - 1)
+    flags = decisions(slide[0] - 1, prev_states.shape[2])
     mods = modulation(timesteps[0], w_time, w_ada[0])
     opening = prev_states[0]
     field = opening.astype(BF16)
 
     for bit in reversed(range(bits)):
         other = swap(field, 1 << bit)
+        if bit == bits - 2:
+            weights = load(weights[:2]) + weights[2:]
         if bit == bits - 1:
             moved = swap(opening, 1)
             other, mods = together(other, mods)
@@ -407,7 +440,9 @@
             if first and bit + 1 < bits - 1:
                 moved = swap(opening, 2 << bit)
                 opening = pick(flags, bits + bit + 1, opening, moved)
-            before, total, sent = add_block(flags, 2 * bits + bit, before, total, other)
+            before, sent, total = add_block(
+                flags, 2 * bits + bit, before, total, other, bit + 2 < bits
+            )
         other = swap(sent, count // 2)
         field = add_last(
             flags, 3 * bits - 1, before, other, (opening, inc) if final else (opening,),

time: 106 us -> 101 us (0.953)
  Pallas kernels: 47 us -> 40 us
  waiting for transfers between devices: 33.7 us -> 37.9 us
  starting transfers between devices: 21.5 us -> 19.1 us
    pallas_call x12 -> x13, Pallas kernels: 9.11 us -> 3.38 us  [the longest x1 2.14 us: load(): pl.pallas_call(load_kernel, in_specs=[pl.BlockSpec(memory_space=pltpu.HBM...]
    ppermute x12, waiting for transfers between devices: 32.4 us -> 36.5 us  [swap(): return lax.ppermute(x, 'win', [(i, i ^ distance) for i in range(count)])]
    ppermute x12, starting transfers between devices: 21.4 us -> 19 us  [swap(): return lax.ppermute(x, 'win', [(i, i ^ distance) for i in range(count)])]
    pallas_call x2, Pallas kernels: 34.3 us -> 33 us  [sweep(): pl.pallas_call(functools.partial(kernel, halo_right, halo_left), in_specs...]
  transfers between devices with their start and end apart: 14 -> 14, of which waited for: 10 -> 10; matrix products, arithmetic and copies ran while one was open for 0% -> 0% of each run, Pallas kernels for 24% -> 23%
where the time goes in v1:
time: 101 us; the launch traced here: 100 us
  Pallas kernels  40 us (40%)
  waiting for transfers between devices  37.9 us (38%)
  starting transfers between devices  19.1 us (19%)
  between operations  2.12 us (2%)
  other arithmetic  1.27 us (1%)
    ppermute x12, waiting for transfers between devices, swap(): return lax.ppermute(x, 'win', [(i, i ^ distance) for i in range(count)])  36.5 us
    pallas_call x2, Pallas kernels, sweep(): pl.pallas_call(functools.partial(kernel, halo_right, halo_left), in_specs...  33 us
    ppermute x12, starting transfers between devices, swap(): return lax.ppermute(x, 'win', [(i, i ^ distance) for i in range(count)])  19 us
    pallas_call x1, Pallas kernels, modulation(): pl.pallas_call(modulation_kernel, in_specs=[vmem, hbm, hbm], out_specs=vm...  3.6 us
    pallas_call x1, Pallas kernels, load(): pl.pallas_call(load_kernel, in_specs=[pl.BlockSpec(memory_space=pltpu.HBM...  2.14 us
  transfers between devices with their start and end apart: 14, of which 10 were waited for; matrix products, arithmetic and copies ran while one was open for 0% of the time, Pallas kernels for 23%

profile of v1, /device:TPU:0, one launch (start us, length us, event | category | flops | bytes accessed | tf_op | source)
XLA Modules:
  0.0 100.5 jit_solution(15310958526565277836)
XLA Ops:
  0.0 1.0 bitcast_convert_fusion.own_ref
  1.0 4.1 %collective-permute-start = (bf16[512,128]{1,0:T(8,128)(2,1)S(1)}, bf16[512,128]{1,0:T(8,128)(2,1)S(1)}, u32[]{:S(2)}, u32[]{:S(2)}) collective-permute-start(bf16[512,128]{1,0:T(8,128)(2,1)S(1)} %bitcast_convert_fusion.own_ref), channel_id=1, source_target_pairs={{0,8},{2,10},{4,12},{6,14},{8,0},{10,2},{12,4},{14,6},{1,9},{3,11}... | collective-permute-start | bytes 393224 | tf_op jit(solution)/shard_map/ppermute | solution.py:327
  5.1 1.5 %collective-permute-start.2 = (f32[512,128]{1,0:T(8,128)}, f32[512,128]{1,0:T(8,128)S(1)}, u32[]{:S(2)}, u32[]{:S(2)}) collective-permute-start(f32[512,128]{1,0:T(8,128)} %bitcast.10), channel_id=1, source_target_pairs={{0,2},{2,0},{4,6},{6,4},{8,10},{10,8},{12,14},{14,12},{1,3},{3,1},... | collective-permute-start | bytes 786440 | tf_op jit(solution)/shard_map/ppermute | solution.py:327
  7.3 0.1 compare_select_fusion
  8.2 3.6 %modulation.1.refs_2_.mods_ref = f32[6,8,768]{2,1,0:T(8,128)S(1)} custom-call(bf16[8,256]{1,0:T(8,128)(2,1)S(1)} %broadcast_in_dim.7.emb_ref, bf16[256,768]{1,0:T(8,128)(2,1)} %w_time_hbm.1, bf16[768,4608]{1,0:T(8,128)(2,1)} %bitcast.12), custom_call_target="tpu_custom_call" | custom-call | flops 56623104 | bytes 7077888 | tf_op jit(solution)/shard_map/modulation/pallas_call | solution.py:115
  11.8 0.1 add_convert_fusion
  12.0 1.6 %collective-permute-start.1 = (bf16[512,128]{1,0:T(8,128)(2,1)S(1)}, bf16[512,128]{1,0:T(8,128)(2,1)S(1)}, u32[]{:S(2)}, u32[]{:S(2)}) collective-permute-start(bf16[512,128]{1,0:T(8,128)(2,1)S(1)} %shard_map.118.own_ref), channel_id=1, source_target_pairs={{0,4},{2,6},{4,0},{6,2},{8,12},{10,14},{12,8},{14,10},{1,5},{3,7},... | collective-permute-start | bytes 393224 | tf_op jit(solution)/shard_map/ppermute | solution.py:327
  13.6 3.4 %collective-permute-done.1.other_ref = bf16[512,128]{1,0:T(8,128)(2,1)S(1)} collective-permute-done((bf16[512,128]{1,0:T(8,128)(2,1)S(1)}, bf16[512,128]{1,0:T(8,128)(2,1)S(1)}, u32[]{:S(2)}, u32[]{:S(2)}) %collective-permute-start.1) | collective-permute-done | bytes 131104 | tf_op jit(solution)/shard_map/ppermute | solution.py:327
  17.0 1.2 %collective-permute-start.3 = (bf16[512,128]{1,0:T(8,128)(2,1)S(1)}, bf16[512,128]{1,0:T(8,128)(2,1)S(1)}, u32[]{:S(2)}, u32[]{:S(2)}) collective-permute-start(bf16[512,128]{1,0:T(8,128)(2,1)S(1)} %shard_map.119.own_ref), channel_id=1, source_target_pairs={{0,2},{2,0},{4,6},{6,4},{8,10},{10,8},{12,14},{14,12},{1,3},{3,1},... | collective-permute-start | bytes 393224 | tf_op jit(solution)/shard_map/ppermute | solution.py:327
  18.2 3.9 %collective-permute-done.3.other_ref = bf16[512,128]{1,0:T(8,128)(2,1)S(1)} collective-permute-done((bf16[512,128]{1,0:T(8,128)(2,1)S(1)}, bf16[512,128]{1,0:T(8,128)(2,1)S(1)}, u32[]{:S(2)}, u32[]{:S(2)}) %collective-permute-start.3) | collective-permute-done | bytes 131104 | tf_op jit(solution)/shard_map/ppermute | solution.py:327
  22.1 0.1 collective-permute-start.4
  22.8 2.1 %load.1 = (bf16[128,768]{1,0:T(8,128)(2,1)S(1)}, bf16[768,2304]{1,0:T(8,128)(2,1)S(1)}) custom-call(bf16[128,768]{1,0:T(8,128)(2,1)} %refs_0_.1, bf16[768,2304]{1,0:T(8,128)(2,1)} %bitcast.13), custom_call_target="tpu_custom_call" | custom-call | bytes 3735552 | tf_op jit(solution)/shard_map/load/pallas_call | solution.py:90
  25.0 2.4 %collective-permute-start.5 = (f32[512,128]{1,0:T(8,128)S(1)}, f32[512,128]{1,0:T(8,128)S(1)}, u32[]{:S(2)}, u32[]{:S(2)}) collective-permute-start(f32[512,128]{1,0:T(8,128)S(1)} %shard_map.121.own_ref), channel_id=1, source_target_pairs={{0,8},{2,10},{4,12},{6,14},{8,0},{10,2},{12,4},{14,6},{1,9},{3,11}... | collective-permute-start | bytes 786440 | tf_op jit(solution)/shard_map/ppermute | solution.py:327
  27.5 16.7 %first_sweep.1 = (f32[512,128]{1,0:T(8,128)S(1)}, bf16[768,768]{1,0:T(8,128)(2,1)S(1)}, bf16[768,3072]{1,0:T(8,128)(2,1)S(1)}, bf16[3072,768]{1,0:T(8,128)(2,1)S(1)}, bf16[768,128]{1,0:T(8,128)(2,1)S(1)}) custom-call(bf16[512,128]{1,0:T(8,128)(2,1)S(1)} %shard_map.120.refs_0_, bf16[512,128]{1,0:T(8,128)(2,1)S(1)} %collective-permute-done.4.refs_1_, ...), custom_call_target="tpu_custom_call" | custom-call | flops 7247757312 | bytes 14548992 | tf_op jit(solution)/shard_map/first_sweep/pallas_call | solution.py:294
  44.2 1.6 %collective-permute-start.6 = (bf16[512,128]{1,0:T(8,128)(2,1)S(1)}, bf16[512,128]{1,0:T(8,128)(2,1)S(1)}, u32[]{:S(2)}, u32[]{:S(2)}) collective-permute-start(bf16[512,128]{1,0:T(8,128)(2,1)S(1)} %convert_element_type.31), channel_id=1, source_target_pairs={{0,2},{2,0},{4,6},{6,4},{8,10},{10,8},{12,14},{14,12},{1,3},{3,1},... | collective-permute-start | bytes 393224 | tf_op jit(solution)/shard_map/ppermute | solution.py:327
  45.7 4.1 %collective-permute-done.6.refs_1_ = bf16[512,128]{1,0:T(8,128)(2,1)S(1)} collective-permute-done((bf16[512,128]{1,0:T(8,128)(2,1)S(1)}, bf16[512,128]{1,0:T(8,128)(2,1)S(1)}, u32[]{:S(2)}, u32[]{:S(2)}) %collective-permute-start.6) | collective-permute-done | bytes 131104 | tf_op jit(solution)/shard_map/ppermute | solution.py:327
  49.9 1.8 %collective-permute-start.7 = (bf16[512,128]{1,0:T(8,128)(2,1)S(1)}, bf16[512,128]{1,0:T(8,128)(2,1)S(1)}, u32[]{:S(2)}, u32[]{:S(2)}) collective-permute-start(bf16[512,128]{1,0:T(8,128)(2,1)S(1)} %get-tuple-element.41), channel_id=1, source_target_pairs={{0,4},{2,6},{4,0},{6,2},{8,12},{10,14},{12,8},{14,10},{1,5},{3,7},... | collective-permute-start | bytes 393224 | tf_op jit(solution)/shard_map/ppermute | solution.py:327
  51.7 0.4 collective-permute-start.9
  52.1 4.2 %collective-permute-done.7.refs_2_ = bf16[512,128]{1,0:T(8,128)(2,1)S(1)} collective-permute-done((bf16[512,128]{1,0:T(8,128)(2,1)S(1)}, bf16[512,128]{1,0:T(8,128)(2,1)S(1)}, u32[]{:S(2)}, u32[]{:S(2)}) %collective-permute-start.7) | collective-permute-done | bytes 131104 | tf_op jit(solution)/shard_map/ppermute | solution.py:327
  56.4 0.6 collective-permute-start.8
  57.0 5.8 %collective-permute-done.9.other_ref = f32[512,128]{1,0:T(8,128)S(1)} collective-permute-done((f32[512,128]{1,0:T(8,128)S(1)}, f32[512,128]{1,0:T(8,128)S(1)}, u32[]{:S(2)}, u32[]{:S(2)}) %collective-permute-start.9) | collective-permute-done | bytes 262176 | tf_op jit(solution)/shard_map/ppermute | solution.py:327
  62.9 1.2 %collective-permute-done.8.other_ref = bf16[512,128]{1,0:T(8,128)(2,1)S(1)} collective-permute-done((bf16[512,128]{1,0:T(8,128)(2,1)S(1)}, bf16[512,128]{1,0:T(8,128)(2,1)S(1)}, u32[]{:S(2)}, u32[]{:S(2)}) %collective-permute-start.8) | collective-permute-done | bytes 131104 | tf_op jit(solution)/shard_map/ppermute | solution.py:327
  64.1 0.1 collective-permute-start.10
  64.2 1.3 %collective-permute-done.10.halo_ref = bf16[512,128]{1,0:T(8,128)(2,1)S(1)} collective-permute-done((bf16[512,128]{1,0:T(8,128)(2,1)S(1)}, bf16[512,128]{1,0:T(8,128)(2,1)S(1)}, u32[]{:S(2)}, u32[]{:S(2)}) %collective-permute-start.10) | collective-permute-done | bytes 131104 | tf_op jit(solution)/shard_map/ppermute | solution.py:318
  65.5 16.3 %sweep.1.refs_0_.refs_1_ = f32[512,128]{1,0:T(8,128)S(1)} custom-call(bf16[512,128]{1,0:T(8,128)(2,1)S(1)} %shard_map.126.own_ref, bf16[512,128]{1,0:T(8,128)(2,1)S(1)} %collective-permute-done.10.halo_ref, f32[6,8,768]{2,1,0:T(8,128)S(1)} %modulation.1.refs_2_.mods_ref, f32[1]{0:T(128)S(6)} %copy.14.refs_3_.step_ref, ...), custom_call_target="tpu_custom_call" | custom-call | flops 7247757312 | bytes 14548992 | tf_op jit(solution)/shard_map/sweep/pallas_call | solution.py:294
  81.9 1.8 %collective-permute-start.11 = (bf16[512,128]{1,0:T(8,128)(2,1)S(1)}, bf16[512,128]{1,0:T(8,128)(2,1)S(1)}, u32[]{:S(2)}, u32[]{:S(2)}) collective-permute-start(bf16[512,128]{1,0:T(8,128)(2,1)S(1)} %convert_element_type.32), channel_id=1, source_target_pairs={{0,2},{2,0},{4,6},{6,4},{8,10},{10,8},{12,14},{14,12},{1,3},{3,1},... | collective-permute-start | bytes 393224 | tf_op jit(solution)/shard_map/ppermute | solution.py:327
  83.7 3.9 %collective-permute-done.11.refs_1_ = bf16[512,128]{1,0:T(8,128)(2,1)S(1)} collective-permute-done((bf16[512,128]{1,0:T(8,128)(2,1)S(1)}, bf16[512,128]{1,0:T(8,128)(2,1)S(1)}, u32[]{:S(2)}, u32[]{:S(2)}) %collective-permute-start.11) | collective-permute-done | bytes 131104 | tf_op jit(solution)/shard_map/ppermute | solution.py:327
  87.6 0.2 collective-permute-start.12
  87.7 4.9 %collective-permute-done.12.refs_2_ = bf16[512,128]{1,0:T(8,128)(2,1)S(1)} collective-permute-done((bf16[512,128]{1,0:T(8,128)(2,1)S(1)}, bf16[512,128]{1,0:T(8,128)(2,1)S(1)}, u32[]{:S(2)}, u32[]{:S(2)}) %collective-permute-start.12) | collective-permute-done | bytes 131104 | tf_op jit(solution)/shard_map/ppermute | solution.py:327
  92.7 1.8 %collective-permute-start.13 = (bf16[512,128]{1,0:T(8,128)(2,1)S(1)}, bf16[512,128]{1,0:T(8,128)(2,1)S(1)}, u32[]{:S(2)}, u32[]{:S(2)}) collective-permute-start(bf16[512,128]{1,0:T(8,128)(2,1)S(1)} %get-tuple-element.54), channel_id=1, source_target_pairs={{0,8},{2,10},{4,12},{6,14},{8,0},{10,2},{12,4},{14,6},{1,9},{3,11}... | collective-permute-start | bytes 393224 | tf_op jit(solution)/shard_map/ppermute | solution.py:327
  94.5 5.2 %collective-permute-done.13.other_ref = bf16[512,128]{1,0:T(8,128)(2,1)S(1)} collective-permute-done((bf16[512,128]{1,0:T(8,128)(2,1)S(1)}, bf16[512,128]{1,0:T(8,128)(2,1)S(1)}, u32[]{:S(2)}, u32[]{:S(2)}) %collective-permute-start.13) | collective-permute-done | bytes 131104 | tf_op jit(solution)/shard_map/ppermute | solution.py:327
  99.7 0.8 shard_map.129
  (24 shorter events, 0.7 us)
Async XLA Ops:
  1.0 10.9 %collective-permute-start = (bf16[512,128]{1,0:T(8,128)(2,1)S(1)}, bf16[512,128]{1,0:T(8,128)(2,1)S(1)}, u32[]{:S(2)}, u32[]{:S(2)}) collective-permute-start(bf16[512,128]{1,0:T(8,128)(2,1)S(1)} %bitcast_convert_fusion.own_ref), channel_id=1, source_target_pairs={{0,8},{2,10},{4,12},{6,14},{8,0},{10,2},{12,4},{14,6},{1,9},{3,11}... | collective-permute-start | bytes 393224 | tf_op jit(solution)/shard_map/ppermute | solution.py:327
  5.1 13.1 %collective-permute-start.2 = (f32[512,128]{1,0:T(8,128)}, f32[512,128]{1,0:T(8,128)S(1)}, u32[]{:S(2)}, u32[]{:S(2)}) collective-permute-start(f32[512,128]{1,0:T(8,128)} %bitcast.10), channel_id=1, source_target_pairs={{0,2},{2,0},{4,6},{6,4},{8,10},{10,8},{12,14},{14,12},{1,3},{3,1},... | collective-permute-start | bytes 786440 | tf_op jit(solution)/shard_map/ppermute | solution.py:327
  8.2 16.8 %copy-start = (f32[1,512,128]{2,1,0:T(8,128)S(1)}, f32[1,512,128]{2,1,0:T(8,128)}, u32[]{:S(2)}) copy-start(f32[1,512,128]{2,1,0:T(8,128)} %param.12) | copy-start | bytes 786436
  12.0 5.0 %collective-permute-start.1 = (bf16[512,128]{1,0:T(8,128)(2,1)S(1)}, bf16[512,128]{1,0:T(8,128)(2,1)S(1)}, u32[]{:S(2)}, u32[]{:S(2)}) collective-permute-start(bf16[512,128]{1,0:T(8,128)(2,1)S(1)} %shard_map.118.own_ref), channel_id=1, source_target_pairs={{0,4},{2,6},{4,0},{6,2},{8,12},{10,14},{12,8},{14,10},{1,5},{3,7},... | collective-permute-start | bytes 393224 | tf_op jit(solution)/shard_map/ppermute | solution.py:327
  17.0 5.0 %collective-permute-start.3 = (bf16[512,128]{1,0:T(8,128)(2,1)S(1)}, bf16[512,128]{1,0:T(8,128)(2,1)S(1)}, u32[]{:S(2)}, u32[]{:S(2)}) collective-permute-start(bf16[512,128]{1,0:T(8,128)(2,1)S(1)} %shard_map.119.own_ref), channel_id=1, source_target_pairs={{0,2},{2,0},{4,6},{6,4},{8,10},{10,8},{12,14},{14,12},{1,3},{3,1},... | collective-permute-start | bytes 393224 | tf_op jit(solution)/shard_map/ppermute | solution.py:327
  22.1 5.3 %collective-permute-start.4 = (bf16[512,128]{1,0:T(8,128)(2,1)S(1)}, bf16[512,128]{1,0:T(8,128)(2,1)S(1)}, u32[]{:S(2)}, u32[]{:S(2)}) collective-permute-start(bf16[512,128]{1,0:T(8,128)(2,1)S(1)} %shard_map.120.refs_0_), channel_id=1, source_target_pairs={{0,1},{1,0},{2,3},{3,2},{4,5},{5,4},{6,7},{7,6},{8,9},{9,8},{10,11... | collective-permute-start | bytes 393224 | tf_op jit(solution)/shard_map/ppermute | solution.py:318
  25.0 19.1 %collective-permute-start.5 = (f32[512,128]{1,0:T(8,128)S(1)}, f32[512,128]{1,0:T(8,128)S(1)}, u32[]{:S(2)}, u32[]{:S(2)}) collective-permute-start(f32[512,128]{1,0:T(8,128)S(1)} %shard_map.121.own_ref), channel_id=1, source_target_pairs={{0,8},{2,10},{4,12},{6,14},{8,0},{10,2},{12,4},{14,6},{1,9},{3,11}... | collective-permute-start | bytes 786440 | tf_op jit(solution)/shard_map/ppermute | solution.py:327
  44.2 5.7 %collective-permute-start.6 = (bf16[512,128]{1,0:T(8,128)(2,1)S(1)}, bf16[512,128]{1,0:T(8,128)(2,1)S(1)}, u32[]{:S(2)}, u32[]{:S(2)}) collective-permute-start(bf16[512,128]{1,0:T(8,128)(2,1)S(1)} %convert_element_type.31), channel_id=1, source_target_pairs={{0,2},{2,0},{4,6},{6,4},{8,10},{10,8},{12,14},{14,12},{1,3},{3,1},... | collective-permute-start | bytes 393224 | tf_op jit(solution)/shard_map/ppermute | solution.py:327
  49.9 6.4 %collective-permute-start.7 = (bf16[512,128]{1,0:T(8,128)(2,1)S(1)}, bf16[512,128]{1,0:T(8,128)(2,1)S(1)}, u32[]{:S(2)}, u32[]{:S(2)}) collective-permute-start(bf16[512,128]{1,0:T(8,128)(2,1)S(1)} %get-tuple-element.41), channel_id=1, source_target_pairs={{0,4},{2,6},{4,0},{6,2},{8,12},{10,14},{12,8},{14,10},{1,5},{3,7},... | collective-permute-start | bytes 393224 | tf_op jit(solution)/shard_map/ppermute | solution.py:327
  51.7 11.1 %collective-permute-start.9 = (f32[512,128]{1,0:T(8,128)S(1)}, f32[512,128]{1,0:T(8,128)S(1)}, u32[]{:S(2)}, u32[]{:S(2)}) collective-permute-start(f32[512,128]{1,0:T(8,128)S(1)} %shard_map.124.own_ref), channel_id=1, source_target_pairs={{0,4},{2,6},{4,0},{6,2},{8,12},{10,14},{12,8},{14,10},{1,5},{3,7},... | collective-permute-start | bytes 786440 | tf_op jit(solution)/shard_map/ppermute | solution.py:327
  56.4 7.7 %collective-permute-start.8 = (bf16[512,128]{1,0:T(8,128)(2,1)S(1)}, bf16[512,128]{1,0:T(8,128)(2,1)S(1)}, u32[]{:S(2)}, u32[]{:S(2)}) collective-permute-start(bf16[512,128]{1,0:T(8,128)(2,1)S(1)} %get-tuple-element.43), channel_id=1, source_target_pairs={{0,8},{2,10},{4,12},{6,14},{8,0},{10,2},{12,4},{14,6},{1,9},{3,11}... | collective-permute-start | bytes 393224 | tf_op jit(solution)/shard_map/ppermute | solution.py:327
  64.1 1.4 %collective-permute-start.10 = (bf16[512,128]{1,0:T(8,128)(2,1)S(1)}, bf16[512,128]{1,0:T(8,128)(2,1)S(1)}, u32[]{:S(2)}, u32[]{:S(2)}) collective-permute-start(bf16[512,128]{1,0:T(8,128)(2,1)S(1)} %shard_map.126.own_ref), channel_id=1, source_target_pairs={{0,1},{1,0},{2,3},{3,2},{4,5},{5,4},{6,7},{7,6},{8,9},{9,8},{10,11... | collective-permute-start | bytes 393224 | tf_op jit(solution)/shard_map/ppermute | solution.py:318
  81.9 5.6 %collective-permute-start.11 = (bf16[512,128]{1,0:T(8,128)(2,1)S(1)}, bf16[512,128]{1,0:T(8,128)(2,1)S(1)}, u32[]{:S(2)}, u32[]{:S(2)}) collective-permute-start(bf16[512,128]{1,0:T(8,128)(2,1)S(1)} %convert_element_type.32), channel_id=1, source_target_pairs={{0,2},{2,0},{4,6},{6,4},{8,10},{10,8},{12,14},{14,12},{1,3},{3,1},... | collective-permute-start | bytes 393224 | tf_op jit(solution)/shard_map/ppermute | solution.py:327
  87.6 5.0 %collective-permute-start.12 = (bf16[512,128]{1,0:T(8,128)(2,1)S(1)}, bf16[512,128]{1,0:T(8,128)(2,1)S(1)}, u32[]{:S(2)}, u32[]{:S(2)}) collective-permute-start(bf16[512,128]{1,0:T(8,128)(2,1)S(1)} %get-tuple-element.52), channel_id=1, source_target_pairs={{0,4},{2,6},{4,0},{6,2},{8,12},{10,14},{12,8},{14,10},{1,5},{3,7},... | collective-permute-start | bytes 393224 | tf_op jit(solution)/shard_map/ppermute | solution.py:327
  92.7 7.0 %collective-permute-start.13 = (bf16[512,128]{1,0:T(8,128)(2,1)S(1)}, bf16[512,128]{1,0:T(8,128)(2,1)S(1)}, u32[]{:S(2)}, u32[]{:S(2)}) collective-permute-start(bf16[512,128]{1,0:T(8,128)(2,1)S(1)} %get-tuple-element.54), channel_id=1, source_target_pairs={{0,8},{2,10},{4,12},{6,14},{8,0},{10,2},{12,4},{14,6},{1,9},{3,11}... | collective-permute-start | bytes 393224 | tf_op jit(solution)/shard_map/ppermute | solution.py:327

commit v2 on v1

--- a/solution.py
+++ b/solution.py
@@ -366,39 +366,59 @@
     return small_call(kernel, (flags, own, other), jax.ShapeDtypeStruct(own.shape, own.dtype))
 
 
-def add_block(flags, flag, before, total, other, more):
+def add_block(flags, flag, before, total, other, send, more):
     def kernel(flags_ref, *refs):
         refs = list(refs)
         start = refs.pop(0)[...] if before is not None else 0.0
-        sums = refs[0][...]
-        arrived = refs[1][...].astype(F32)
+        sums = refs.pop(0)[...]
+        arrived = refs.pop(0)[...].astype(F32)
         above = flags_ref[flag:flag + 1, :] != 0
-        refs[2][...] = start + jnp.where(above, arrived, 0.0)
+        refs.pop(0)[...] = start + jnp.where(above, arrived, 0.0)
         sums = sums + arrived
-        refs[3][...] = sums.astype(BF16)
-        if more:
-            refs[4][...] = sums
+        for ref in refs:
+            ref[...] = sums.astype(ref.dtype)
 
     wide = jax.ShapeDtypeStruct(total.shape, F32)
     narrow = jax.ShapeDtypeStruct(total.shape, BF16)
     args = (flags,) + (() if before is None else (before,)) + (total, other)
-    out = small_call(kernel, args, (wide, narrow) + ((wide,) if more else ()))
-    return out if more else (*out, None)
-
-
-def add_last(flags, flag, before, other, extra, kind):
-    def kernel(flags_ref, before_ref, other_ref, *refs):
+    outs = (wide,) + ((narrow,) if send else ()) + ((wide,) if more else ())
+    out = small_call(kernel, args, outs)
+    return out[0], out[1] if send else None, out[-1] if more else None
+
+
+def offer(flags, bits, total, opening):
+    def kernel(flags_ref, total_ref, opening_ref, out_ref):
+        above = flags_ref[3 * bits - 1:3 * bits, :] != 0
+        known = flags_ref[2 * bits - 1:2 * bits, :] != 0
+        start = opening_ref[...]
+        sums = total_ref[...] + jnp.where(known, start, 0.0)
+        out_ref[...] = jnp.where(above, start, sums).astype(BF16)
+
+    out = jax.ShapeDtypeStruct(total.shape, BF16)
+    return small_call(kernel, (flags, total, opening), out)
+
+
+def advance(flags, bits, before, other, opening):
+    def kernel(flags_ref, before_ref, other_ref, opening_ref, out_ref):
+        above = flags_ref[3 * bits - 1:3 * bits, :] != 0
+        known = flags_ref[2 * bits - 1:2 * bits, :] != 0
+        start = jnp.where(known, opening_ref[...], 0.0)
+        wanted = above | jnp.logical_not(known)
+        total = before_ref[...] + jnp.where(wanted, other_ref[...].astype(F32), 0.0)
+        out_ref[...] = (start + total).astype(BF16)
+
+    out = jax.ShapeDtypeStruct(before.shape, BF16)
+    return small_call(kernel, (flags, before, other, opening), out)
+
+
+def close(flags, flag, before, other, opening, inc):
+    def kernel(flags_ref, before_ref, other_ref, opening_ref, inc_ref, out_ref):
         above = flags_ref[flag:flag + 1, :] != 0
-        mine = jnp.where(above, other_ref[...].astype(F32), 0.0)
-        total = before_ref[...] + mine
-        for ref in refs[:-1]:
-            total = total + ref[...]
-        refs[-1][...] = total.astype(kind)
-
-    return small_call(
-        kernel, (flags, before, other) + extra,
-        jax.ShapeDtypeStruct(before.shape, kind),
-    )
+        total = before_ref[...] + jnp.where(above, other_ref[...].astype(F32), 0.0)
+        out_ref[...] = opening_ref[...] + (total + inc_ref[...])
+
+    out = jax.ShapeDtypeStruct(inc.shape, F32)
+    return small_call(kernel, (flags, before, other, opening, inc), out)
 
 
 def window_steps(
@@ -414,40 +434,49 @@
     opening = prev_states[0]
     field = opening.astype(BF16)
 
+    inner = range(1, bits - 1)
     for bit in reversed(range(bits)):
         other = swap(field, 1 << bit)
         if bit == bits - 2:
-            weights = load(weights[:2]) + weights[2:]
+            other, mods = together(other, mods)
         if bit == bits - 1:
             moved = swap(opening, 1)
-            other, mods = together(other, mods)
+            weights = load(weights[:2]) + weights[2:]
         if bit == 0:
             field, opening, moved = together(field, opening, moved)
             opening = pick(flags, bits, opening, moved)
-            moved = swap(opening, count // 2)
+            if inner:
+                moved = swap(opening, 1 << inner[0])
         field = pick(flags, bit, field, other)
     for sweep_index in range(SWEEPS):
-        first = sweep_index == 0
-        final = sweep_index == SWEEPS - 1
+        first, final = sweep_index == 0, sweep_index == SWEEPS - 1
         halo, right, left = rim_of_neighbours(field)
+        if final:
+            field, opening = together(field, opening)
+            moved = swap(opening, count // 2)
         inc, weights = sweep(field, halo, right, left, mods, step_sizes, weights, first)
-        if first:
+        if first and inner:
+            inc, opening, moved = together(inc, opening, moved)
+            opening = pick(flags, bits + inner[0], opening, moved)
+        if final:
             inc, opening, moved = together(inc, opening, moved)
             opening = pick(flags, 2 * bits - 1, opening, moved)
         before, total, sent = None, inc, inc.astype(BF16)
         for bit in range(bits - 1):
             other = swap(sent, 1 << bit)
-            if first and bit + 1 < bits - 1:
-                moved = swap(opening, 2 << bit)
-                opening = pick(flags, bits + bit + 1, opening, moved)
+            if first and bit + 2 in inner:
+                moved = swap(opening, 4 << bit)
+                opening = pick(flags, bits + bit + 2, opening, moved)
             before, sent, total = add_block(
-                flags, 2 * bits + bit, before, total, other, bit + 2 < bits
+                flags, 2 * bits + bit, before, total, other,
+                send=bit + 2 < bits or final, more=bit + 2 < bits or not final,
             )
-        other = swap(sent, count // 2)
-        field = add_last(
-            flags, 3 * bits - 1, before, other, (opening, inc) if final else (opening,),
-            F32 if final else BF16,
-        )
+        if final:
+            other = swap(sent, count // 2)
+            field = close(flags, 3 * bits - 1, before, other, opening, inc)
+        else:
+            other = swap(offer(flags, bits, total, opening), count // 2)
+            field = advance(flags, bits, before, other, opening)
     return field[None]
 
 

time: 101 us -> 98.7 us (0.977)
  waiting for transfers between devices: 37.9 us -> 33.1 us
  starting transfers between devices: 19.1 us -> 22 us
    ppermute x12, waiting for transfers between devices: 36.5 us -> 33.1 us  [swap(): return lax.ppermute(x, 'win', [(i, i ^ distance) for i in range(count)])]
    ppermute x12, starting transfers between devices: 19 us -> 21.8 us  [swap(): return lax.ppermute(x, 'win', [(i, i ^ distance) for i in range(count)])]
    ppermute x2, waiting for transfers between devices: 1.34 us -> 0.01 us  [rim_of_neighbours(): other = lax.ppermute(field, 'gx', [(0, 1), (1, 0)])]
  transfers between devices with their start and end apart: 14 -> 14, of which waited for: 10 -> 9; matrix products, arithmetic and copies ran while one was open for 0% -> 0% of each run, Pallas kernels for 23% -> 39%
where the time goes in v2:
time: 98.7 us; the launch traced here: 98.5 us
  Pallas kernels  40 us (41%)
  waiting for transfers between devices  33.1 us (34%)
  starting transfers between devices  22 us (22%)
  between operations  2.13 us (2%)
  other arithmetic  1.27 us (1%)
    ppermute x12, waiting for transfers between devices, swap(): return lax.ppermute(x, 'win', [(i, i ^ distance) for i in range(count)])  33.1 us
    pallas_call x2, Pallas kernels, sweep(): pl.pallas_call(functools.partial(kernel, halo_right, halo_left), in_specs...  33 us
    ppermute x12, starting transfers between devices, swap(): return lax.ppermute(x, 'win', [(i, i ^ distance) for i in range(count)])  21.8 us
    pallas_call x1, Pallas kernels, modulation(): pl.pallas_call(modulation_kernel, in_specs=[vmem, hbm, hbm], out_specs=vm...  3.6 us
    pallas_call x1, Pallas kernels, load(): pl.pallas_call(load_kernel, in_specs=[pl.BlockSpec(memory_space=pltpu.HBM...  2.14 us
  transfers between devices with their start and end apart: 14, of which 9 were waited for; matrix products, arithmetic and copies ran while one was open for 0% of the time, Pallas kernels for 39%

profile of v2, /device:TPU:0, one launch (start us, length us, event | category | flops | bytes accessed | tf_op | source)
XLA Modules:
  0.0 98.5 jit_solution(7223919459544689490)
XLA Ops:
  0.0 1.0 bitcast_convert_fusion.own_ref
  1.0 4.1 %collective-permute-start = (bf16[512,128]{1,0:T(8,128)(2,1)S(1)}, bf16[512,128]{1,0:T(8,128)(2,1)S(1)}, u32[]{:S(2)}, u32[]{:S(2)}) collective-permute-start(bf16[512,128]{1,0:T(8,128)(2,1)S(1)} %bitcast_convert_fusion.own_ref), channel_id=1, source_target_pairs={{0,8},{2,10},{4,12},{6,14},{8,0},{10,2},{12,4},{14,6},{1,9},{3,11}... | collective-permute-start | bytes 393224 | tf_op jit(solution)/shard_map/ppermute | solution.py:327
  5.1 1.5 %collective-permute-start.2 = (f32[512,128]{1,0:T(8,128)}, f32[512,128]{1,0:T(8,128)S(1)}, u32[]{:S(2)}, u32[]{:S(2)}) collective-permute-start(f32[512,128]{1,0:T(8,128)} %bitcast.10), channel_id=1, source_target_pairs={{0,2},{2,0},{4,6},{6,4},{8,10},{10,8},{12,14},{14,12},{1,3},{3,1},... | collective-permute-start | bytes 786440 | tf_op jit(solution)/shard_map/ppermute | solution.py:327
  7.3 0.1 compare_select_fusion
  8.1 0.1 add_convert_fusion
  8.1 3.3 %collective-permute-done.other_ref = bf16[512,128]{1,0:T(8,128)(2,1)S(1)} collective-permute-done((bf16[512,128]{1,0:T(8,128)(2,1)S(1)}, bf16[512,128]{1,0:T(8,128)(2,1)S(1)}, u32[]{:S(2)}, u32[]{:S(2)}) %collective-permute-start) | collective-permute-done | bytes 131104 | tf_op jit(solution)/shard_map/ppermute | solution.py:327
  11.4 0.1 broadcast_in_dim.6.flags_ref
  11.5 0.8 collective-permute-start.1
  12.4 3.6 %modulation.1.refs_2_.mods_ref = f32[6,8,768]{2,1,0:T(8,128)S(1)} custom-call(bf16[8,256]{1,0:T(8,128)(2,1)S(1)} %broadcast_in_dim.7.emb_ref, bf16[256,768]{1,0:T(8,128)(2,1)} %w_time_hbm.1, bf16[768,4608]{1,0:T(8,128)(2,1)} %bitcast.12), custom_call_target="tpu_custom_call" | custom-call | flops 56623104 | bytes 7077888 | tf_op jit(solution)/shard_map/modulation/pallas_call | solution.py:115
  16.0 0.5 collective-permute-done.1.other_ref
  16.6 1.6 %collective-permute-start.3 = (bf16[512,128]{1,0:T(8,128)(2,1)S(1)}, bf16[512,128]{1,0:T(8,128)(2,1)S(1)}, u32[]{:S(2)}, u32[]{:S(2)}) collective-permute-start(bf16[512,128]{1,0:T(8,128)(2,1)S(1)} %shard_map.119.own_ref), channel_id=1, source_target_pairs={{0,2},{2,0},{4,6},{6,4},{8,10},{10,8},{12,14},{14,12},{1,3},{3,1},... | collective-permute-start | bytes 393224 | tf_op jit(solution)/shard_map/ppermute | solution.py:327
  18.2 3.4 %collective-permute-done.3.other_ref = bf16[512,128]{1,0:T(8,128)(2,1)S(1)} collective-permute-done((bf16[512,128]{1,0:T(8,128)(2,1)S(1)}, bf16[512,128]{1,0:T(8,128)(2,1)S(1)}, u32[]{:S(2)}, u32[]{:S(2)}) %collective-permute-start.3) | collective-permute-done | bytes 131104 | tf_op jit(solution)/shard_map/ppermute | solution.py:327
  21.7 0.1 collective-permute-start.4
  22.4 2.1 %load.1 = (bf16[128,768]{1,0:T(8,128)(2,1)S(1)}, bf16[768,2304]{1,0:T(8,128)(2,1)S(1)}) custom-call(bf16[128,768]{1,0:T(8,128)(2,1)} %refs_0_.1, bf16[768,2304]{1,0:T(8,128)(2,1)} %bitcast.13), custom_call_target="tpu_custom_call" | custom-call | bytes 3735552 | tf_op jit(solution)/shard_map/load/pallas_call | solution.py:90
  24.6 1.2 %collective-permute-start.5 = (f32[512,128]{1,0:T(8,128)S(1)}, f32[512,128]{1,0:T(8,128)S(1)}, u32[]{:S(2)}, u32[]{:S(2)}) collective-permute-start(f32[512,128]{1,0:T(8,128)S(1)} %shard_map.121.own_ref), channel_id=1, source_target_pairs={{0,4},{2,6},{4,0},{6,2},{8,12},{10,14},{12,8},{14,10},{1,5},{3,7},... | collective-permute-start | bytes 786440 | tf_op jit(solution)/shard_map/ppermute | solution.py:327
  25.8 16.7 %first_sweep.1 = (f32[512,128]{1,0:T(8,128)S(1)}, bf16[768,768]{1,0:T(8,128)(2,1)S(1)}, bf16[768,3072]{1,0:T(8,128)(2,1)S(1)}, bf16[3072,768]{1,0:T(8,128)(2,1)S(1)}, bf16[768,128]{1,0:T(8,128)(2,1)S(1)}) custom-call(bf16[512,128]{1,0:T(8,128)(2,1)S(1)} %shard_map.120.refs_0_, bf16[512,128]{1,0:T(8,128)(2,1)S(1)} %collective-permute-done.4.refs_1_, ...), custom_call_target="tpu_custom_call" | custom-call | flops 7247757312 | bytes 14548992 | tf_op jit(solution)/shard_map/first_sweep/pallas_call | solution.py:294
  42.5 1.6 %collective-permute-start.6 = (bf16[512,128]{1,0:T(8,128)(2,1)S(1)}, bf16[512,128]{1,0:T(8,128)(2,1)S(1)}, u32[]{:S(2)}, u32[]{:S(2)}) collective-permute-start(bf16[512,128]{1,0:T(8,128)(2,1)S(1)} %convert_element_type.31), channel_id=1, source_target_pairs={{0,2},{2,0},{4,6},{6,4},{8,10},{10,8},{12,14},{14,12},{1,3},{3,1},... | collective-permute-start | bytes 393224 | tf_op jit(solution)/shard_map/ppermute | solution.py:327
  44.1 4.1 %collective-permute-done.6.refs_1_ = bf16[512,128]{1,0:T(8,128)(2,1)S(1)} collective-permute-done((bf16[512,128]{1,0:T(8,128)(2,1)S(1)}, bf16[512,128]{1,0:T(8,128)(2,1)S(1)}, u32[]{:S(2)}, u32[]{:S(2)}) %collective-permute-start.6) | collective-permute-done | bytes 131104 | tf_op jit(solution)/shard_map/ppermute | solution.py:327
  48.3 0.9 collective-permute-start.7
  49.2 4.1 %collective-permute-done.7.refs_2_ = bf16[512,128]{1,0:T(8,128)(2,1)S(1)} collective-permute-done((bf16[512,128]{1,0:T(8,128)(2,1)S(1)}, bf16[512,128]{1,0:T(8,128)(2,1)S(1)}, u32[]{:S(2)}, u32[]{:S(2)}) %collective-permute-start.7) | collective-permute-done | bytes 131104 | tf_op jit(solution)/shard_map/ppermute | solution.py:327
  53.4 3.7 %collective-permute-start.8 = (bf16[512,128]{1,0:T(8,128)(2,1)S(1)}, bf16[512,128]{1,0:T(8,128)(2,1)S(1)}, u32[]{:S(2)}, u32[]{:S(2)}) collective-permute-start(bf16[512,128]{1,0:T(8,128)(2,1)S(1)} %shard_map.125), channel_id=1, source_target_pairs={{0,8},{2,10},{4,12},{6,14},{8,0},{10,2},{12,4},{14,6},{1,9},{3,11}... | collective-permute-start | bytes 393224 | tf_op jit(solution)/shard_map/ppermute | solution.py:327
  57.1 4.4 %collective-permute-done.8.other_ref = bf16[512,128]{1,0:T(8,128)(2,1)S(1)} collective-permute-done((bf16[512,128]{1,0:T(8,128)(2,1)S(1)}, bf16[512,128]{1,0:T(8,128)(2,1)S(1)}, u32[]{:S(2)}, u32[]{:S(2)}) %collective-permute-start.8) | collective-permute-done | bytes 131104 | tf_op jit(solution)/shard_map/ppermute | solution.py:327
  61.6 0.1 collective-permute-start.9
  61.6 1.6 %collective-permute-start.10 = (f32[512,128]{1,0:T(8,128)S(1)}, f32[512,128]{1,0:T(8,128)S(1)}, u32[]{:S(2)}, u32[]{:S(2)}) collective-permute-start(f32[512,128]{1,0:T(8,128)S(1)} %shard_map.124.opening_ref.own_ref), channel_id=1, source_target_pairs={{0,8},{2,10},{4,12},{6,14},{8,0},{10,2},{12,4},{14,6},{1,9},{3,11}... | collective-permute-start | bytes 786440 | tf_op jit(solution)/shard_map/ppermute | solution.py:327
  63.3 16.3 %sweep.1.refs_0_.inc_ref = f32[512,128]{1,0:T(8,128)S(1)} custom-call(bf16[512,128]{1,0:T(8,128)(2,1)S(1)} %shard_map.126.own_ref, bf16[512,128]{1,0:T(8,128)(2,1)S(1)} %collective-permute-done.9.halo_ref, f32[6,8,768]{2,1,0:T(8,128)S(1)} %modulation.1.refs_2_.mods_ref, f32[1]{0:T(128)S(6)} %copy.14.refs_3_.step_ref, ...), custom_call_target="tpu_custom_call" | custom-call | flops 7247757312 | bytes 14548992 | tf_op jit(solution)/shard_map/sweep/pallas_call | solution.py:294
  79.7 1.6 %collective-permute-start.11 = (bf16[512,128]{1,0:T(8,128)(2,1)S(1)}, bf16[512,128]{1,0:T(8,128)(2,1)S(1)}, u32[]{:S(2)}, u32[]{:S(2)}) collective-permute-start(bf16[512,128]{1,0:T(8,128)(2,1)S(1)} %convert_element_type.32), channel_id=1, source_target_pairs={{0,2},{2,0},{4,6},{6,4},{8,10},{10,8},{12,14},{14,12},{1,3},{3,1},... | collective-permute-start | bytes 393224 | tf_op jit(solution)/shard_map/ppermute | solution.py:327
  81.2 4.0 %collective-permute-done.11.refs_1_ = bf16[512,128]{1,0:T(8,128)(2,1)S(1)} collective-permute-done((bf16[512,128]{1,0:T(8,128)(2,1)S(1)}, bf16[512,128]{1,0:T(8,128)(2,1)S(1)}, u32[]{:S(2)}, u32[]{:S(2)}) %collective-permute-start.11) | collective-permute-done | bytes 131104 | tf_op jit(solution)/shard_map/ppermute | solution.py:327
  85.3 1.7 %collective-permute-start.12 = (bf16[512,128]{1,0:T(8,128)(2,1)S(1)}, bf16[512,128]{1,0:T(8,128)(2,1)S(1)}, u32[]{:S(2)}, u32[]{:S(2)}) collective-permute-start(bf16[512,128]{1,0:T(8,128)(2,1)S(1)} %get-tuple-element.60), channel_id=1, source_target_pairs={{0,4},{2,6},{4,0},{6,2},{8,12},{10,14},{12,8},{14,10},{1,5},{3,7},... | collective-permute-start | bytes 393224 | tf_op jit(solution)/shard_map/ppermute | solution.py:327
  87.0 3.4 %collective-permute-done.12.refs_2_ = bf16[512,128]{1,0:T(8,128)(2,1)S(1)} collective-permute-done((bf16[512,128]{1,0:T(8,128)(2,1)S(1)}, bf16[512,128]{1,0:T(8,128)(2,1)S(1)}, u32[]{:S(2)}, u32[]{:S(2)}) %collective-permute-start.12) | collective-permute-done | bytes 131104 | tf_op jit(solution)/shard_map/ppermute | solution.py:327
  90.4 1.4 %collective-permute-start.13 = (bf16[512,128]{1,0:T(8,128)(2,1)S(1)}, bf16[512,128]{1,0:T(8,128)(2,1)S(1)}, u32[]{:S(2)}, u32[]{:S(2)}) collective-permute-start(bf16[512,128]{1,0:T(8,128)(2,1)S(1)} %get-tuple-element.62), channel_id=1, source_target_pairs={{0,8},{2,10},{4,12},{6,14},{8,0},{10,2},{12,4},{14,6},{1,9},{3,11}... | collective-permute-start | bytes 393224 | tf_op jit(solution)/shard_map/ppermute | solution.py:327
  91.9 5.9 %collective-permute-done.13.other_ref = bf16[512,128]{1,0:T(8,128)(2,1)S(1)} collective-permute-done((bf16[512,128]{1,0:T(8,128)(2,1)S(1)}, bf16[512,128]{1,0:T(8,128)(2,1)S(1)}, u32[]{:S(2)}, u32[]{:S(2)}) %collective-permute-start.13) | collective-permute-done | bytes 131104 | tf_op jit(solution)/shard_map/ppermute | solution.py:327
  97.8 0.8 shard_map.130
  (25 shorter events, 0.6 us)
Async XLA Ops:
  1.0 10.4 %collective-permute-start = (bf16[512,128]{1,0:T(8,128)(2,1)S(1)}, bf16[512,128]{1,0:T(8,128)(2,1)S(1)}, u32[]{:S(2)}, u32[]{:S(2)}) collective-permute-start(bf16[512,128]{1,0:T(8,128)(2,1)S(1)} %bitcast_convert_fusion.own_ref), channel_id=1, source_target_pairs={{0,8},{2,10},{4,12},{6,14},{8,0},{10,2},{12,4},{14,6},{1,9},{3,11}... | collective-permute-start | bytes 393224 | tf_op jit(solution)/shard_map/ppermute | solution.py:327
  5.1 13.1 %collective-permute-start.2 = (f32[512,128]{1,0:T(8,128)}, f32[512,128]{1,0:T(8,128)S(1)}, u32[]{:S(2)}, u32[]{:S(2)}) collective-permute-start(f32[512,128]{1,0:T(8,128)} %bitcast.10), channel_id=1, source_target_pairs={{0,2},{2,0},{4,6},{6,4},{8,10},{10,8},{12,14},{14,12},{1,3},{3,1},... | collective-permute-start | bytes 786440 | tf_op jit(solution)/shard_map/ppermute | solution.py:327
  11.5 5.0 %collective-permute-start.1 = (bf16[512,128]{1,0:T(8,128)(2,1)S(1)}, bf16[512,128]{1,0:T(8,128)(2,1)S(1)}, u32[]{:S(2)}, u32[]{:S(2)}) collective-permute-start(bf16[512,128]{1,0:T(8,128)(2,1)S(1)} %shard_map.118.own_ref), channel_id=1, source_target_pairs={{0,4},{2,6},{4,0},{6,2},{8,12},{10,14},{12,8},{14,10},{1,5},{3,7},... | collective-permute-start | bytes 393224 | tf_op jit(solution)/shard_map/ppermute | solution.py:327
  12.4 12.2 %copy-start = (f32[1,512,128]{2,1,0:T(8,128)S(1)}, f32[1,512,128]{2,1,0:T(8,128)}, u32[]{:S(2)}) copy-start(f32[1,512,128]{2,1,0:T(8,128)} %param.12) | copy-start | bytes 786436
  16.6 5.0 %collective-permute-start.3 = (bf16[512,128]{1,0:T(8,128)(2,1)S(1)}, bf16[512,128]{1,0:T(8,128)(2,1)S(1)}, u32[]{:S(2)}, u32[]{:S(2)}) collective-permute-start(bf16[512,128]{1,0:T(8,128)(2,1)S(1)} %shard_map.119.own_ref), channel_id=1, source_target_pairs={{0,2},{2,0},{4,6},{6,4},{8,10},{10,8},{12,14},{14,12},{1,3},{3,1},... | collective-permute-start | bytes 393224 | tf_op jit(solution)/shard_map/ppermute | solution.py:327
  21.7 4.2 %collective-permute-start.4 = (bf16[512,128]{1,0:T(8,128)(2,1)S(1)}, bf16[512,128]{1,0:T(8,128)(2,1)S(1)}, u32[]{:S(2)}, u32[]{:S(2)}) collective-permute-start(bf16[512,128]{1,0:T(8,128)(2,1)S(1)} %shard_map.120.refs_0_), channel_id=1, source_target_pairs={{0,1},{1,0},{2,3},{3,2},{4,5},{5,4},{6,7},{7,6},{8,9},{9,8},{10,11... | collective-permute-start | bytes 393224 | tf_op jit(solution)/shard_map/ppermute | solution.py:318
  24.6 17.9 %collective-permute-start.5 = (f32[512,128]{1,0:T(8,128)S(1)}, f32[512,128]{1,0:T(8,128)S(1)}, u32[]{:S(2)}, u32[]{:S(2)}) collective-permute-start(f32[512,128]{1,0:T(8,128)S(1)} %shard_map.121.own_ref), channel_id=1, source_target_pairs={{0,4},{2,6},{4,0},{6,2},{8,12},{10,14},{12,8},{14,10},{1,5},{3,7},... | collective-permute-start | bytes 786440 | tf_op jit(solution)/shard_map/ppermute | solution.py:327
  42.5 5.7 %collective-permute-start.6 = (bf16[512,128]{1,0:T(8,128)(2,1)S(1)}, bf16[512,128]{1,0:T(8,128)(2,1)S(1)}, u32[]{:S(2)}, u32[]{:S(2)}) collective-permute-start(bf16[512,128]{1,0:T(8,128)(2,1)S(1)} %convert_element_type.31), channel_id=1, source_target_pairs={{0,2},{2,0},{4,6},{6,4},{8,10},{10,8},{12,14},{14,12},{1,3},{3,1},... | collective-permute-start | bytes 393224 | tf_op jit(solution)/shard_map/ppermute | solution.py:327
  48.3 5.0 %collective-permute-start.7 = (bf16[512,128]{1,0:T(8,128)(2,1)S(1)}, bf16[512,128]{1,0:T(8,128)(2,1)S(1)}, u32[]{:S(2)}, u32[]{:S(2)}) collective-permute-start(bf16[512,128]{1,0:T(8,128)(2,1)S(1)} %get-tuple-element.46), channel_id=1, source_target_pairs={{0,4},{2,6},{4,0},{6,2},{8,12},{10,14},{12,8},{14,10},{1,5},{3,7},... | collective-permute-start | bytes 393224 | tf_op jit(solution)/shard_map/ppermute | solution.py:327
  53.4 8.1 %collective-permute-start.8 = (bf16[512,128]{1,0:T(8,128)(2,1)S(1)}, bf16[512,128]{1,0:T(8,128)(2,1)S(1)}, u32[]{:S(2)}, u32[]{:S(2)}) collective-permute-start(bf16[512,128]{1,0:T(8,128)(2,1)S(1)} %shard_map.125), channel_id=1, source_target_pairs={{0,8},{2,10},{4,12},{6,14},{8,0},{10,2},{12,4},{14,6},{1,9},{3,11}... | collective-permute-start | bytes 393224 | tf_op jit(solution)/shard_map/ppermute | solution.py:327
  61.6 1.7 %collective-permute-start.9 = (bf16[512,128]{1,0:T(8,128)(2,1)S(1)}, bf16[512,128]{1,0:T(8,128)(2,1)S(1)}, u32[]{:S(2)}, u32[]{:S(2)}) collective-permute-start(bf16[512,128]{1,0:T(8,128)(2,1)S(1)} %shard_map.126.own_ref), channel_id=1, source_target_pairs={{0,1},{1,0},{2,3},{3,2},{4,5},{5,4},{6,7},{7,6},{8,9},{9,8},{10,11... | collective-permute-start | bytes 393224 | tf_op jit(solution)/shard_map/ppermute | solution.py:318
  61.6 18.0 %collective-permute-start.10 = (f32[512,128]{1,0:T(8,128)S(1)}, f32[512,128]{1,0:T(8,128)S(1)}, u32[]{:S(2)}, u32[]{:S(2)}) collective-permute-start(f32[512,128]{1,0:T(8,128)S(1)} %shard_map.124.opening_ref.own_ref), channel_id=1, source_target_pairs={{0,8},{2,10},{4,12},{6,14},{8,0},{10,2},{12,4},{14,6},{1,9},{3,11}... | collective-permute-start | bytes 786440 | tf_op jit(solution)/shard_map/ppermute | solution.py:327
  79.7 5.6 %collective-permute-start.11 = (bf16[512,128]{1,0:T(8,128)(2,1)S(1)}, bf16[512,128]{1,0:T(8,128)(2,1)S(1)}, u32[]{:S(2)}, u32[]{:S(2)}) collective-permute-start(bf16[512,128]{1,0:T(8,128)(2,1)S(1)} %convert_element_type.32), channel_id=1, source_target_pairs={{0,2},{2,0},{4,6},{6,4},{8,10},{10,8},{12,14},{14,12},{1,3},{3,1},... | collective-permute-start | bytes 393224 | tf_op jit(solution)/shard_map/ppermute | solution.py:327
  85.3 5.0 %collective-permute-start.12 = (bf16[512,128]{1,0:T(8,128)(2,1)S(1)}, bf16[512,128]{1,0:T(8,128)(2,1)S(1)}, u32[]{:S(2)}, u32[]{:S(2)}) collective-permute-start(bf16[512,128]{1,0:T(8,128)(2,1)S(1)} %get-tuple-element.60), channel_id=1, source_target_pairs={{0,4},{2,6},{4,0},{6,2},{8,12},{10,14},{12,8},{14,10},{1,5},{3,7},... | collective-permute-start | bytes 393224 | tf_op jit(solution)/shard_map/ppermute | solution.py:327
  90.4 7.3 %collective-permute-start.13 = (bf16[512,128]{1,0:T(8,128)(2,1)S(1)}, bf16[512,128]{1,0:T(8,128)(2,1)S(1)}, u32[]{:S(2)}, u32[]{:S(2)}) collective-permute-start(bf16[512,128]{1,0:T(8,128)(2,1)S(1)} %get-tuple-element.62), channel_id=1, source_target_pairs={{0,8},{2,10},{4,12},{6,14},{8,0},{10,2},{12,4},{14,6},{1,9},{3,11}... | collective-permute-start | bytes 393224 | tf_op jit(solution)/shard_map/ppermute | solution.py:327
